TPU v7x, 128 devices: a whole 4x4x4 slice. The times are simulated.
128 devices in a mesh: dom: 16 (over z, y), tile: 8 (over x, core).
Axes of the slice: x: 4, y: 4, z: 4, core: 2. Of those that a mesh axis runs over, the one named last changes fastest.
Arguments:
- dof_values: float32 [20, 9, 65536], P(None, None, ('dom', 'tile')), may hold values from -6 to 6
- density: float32 [65536], P(('dom', 'tile')), may hold values from 1 to 3
- lame_lambda: float32 [65536], P(('dom', 'tile')), may hold values from 0.5 to 2
- shear_modulus: float32 [65536], P(('dom', 'tile')), may hold values from 0 to 3, as said below
- jacobian: float32 [3, 3, 65536], P(None, None, ('dom', 'tile')), may hold values from -4 to 4
- normals: float32 [4, 3, 65536], P(None, None, ('dom', 'tile')), may hold values from -4 to 4
- face_scale: float32 [4, 65536], P(None, ('dom', 'tile')), may hold values from 0.5 to 2
- derivative: float32 [3, 20, 20], replicated, may hold values from -1.25 to 1.25
- face_proj: float32 [4, 10, 20], replicated, may hold values from -1.25 to 1.25
- lift_matrix: float32 [4, 20, 10], replicated, may hold values from -2 to 2
- neighbour: int32 [4, 65536], P(None, ('dom', 'tile')), may hold values from 0 to 2399, as said below
- send_face: int32 [1408, 32], P(('dom', 'tile')), may hold values from 0 to 2047
- cluster: int32 [65536], P(('dom', 'tile')), may hold values 0 or 1
- sea_face: int32 [16384, 64], P(('dom', 'tile')), may hold values from -1 to 511, as said below
- sea_cell: int32 [16384, 64], P(('dom', 'tile')), may hold values from 0 to 32767
- height: float32 [1024, 4096], P('dom', 'tile'), may hold values from -4 to 4
- momentum: float32 [2, 1024, 4096], P(None, 'dom', 'tile'), may hold values from -4 to 4
- ocean_depth: float32 [1024, 4096], P('dom', 'tile'), may hold values from 0.5 to 2
Outputs:
- dof_out: float32 [20, 9, 65536], P(None, None, ('dom', 'tile'))
- height_out: float32 [1024, 4096], P('dom', 'tile')
- momentum_out: float32 [2, 1024, 4096], P(None, 'dom', 'tile')
Inputs may be any that keep to these rules, and one draw needn't show every extreme that they name: `neighbour`: an entry below 2048 names local face f * 512 + e of the same device; an entry 2048 + n * 32 + c names slot c of what partner n sends to this device. `send_face`: row s * 11 + n lists local faces f * 512 + e of device s sent to its partner n. `sea_face`: row s * 128 + d lists local elements of device s whose bottom face lies under tile d; rows are live only where (d - s) mod 128 is 0, 1, 8 or 64; live entries come first, the rest are -1; each device's own row is full. `sea_cell`: row d * 128 + s gives, for each slot of device s, the cell i * 512 + j of tile d. `shear_modulus`: zero in a tenth of the elements or so, else positive.
All inputs are finite; a program needn't handle non-finite values. No bound on the sum of `cluster` on one device may be relied on, other than what follows from the above.
Results may differ from a plain program's by a relative error of at most 0.0003.
Values sent between devices are 32-bit elements; how exact they have to be, the bound alone decides.
A program may use at most 64 MiB of HBM per device.

v0:
```python
import jax
import jax.numpy as jnp
from jax import lax
from jax.sharding import PartitionSpec as P

STEPS = 4


STRESS_PAIRS = ((0, 3, 5), (3, 1, 4), (5, 4, 2))
highest = lax.Precision.HIGHEST
step_size = 0.3
wave_rate = 0.45


def extended(shard, sides, width):
    for axis, dim in sides:
        peers, length = (lax.axis_size(axis), shard.shape[dim])
        up = [(i, (i + 1) % peers) for i in range(peers - 1)]
        down = [(j, i) for i, j in up]
        last = lax.slice_in_dim(shard, length - width, length, axis=dim)
        first = lax.slice_in_dim(shard, 0, width, axis=dim)
        before = lax.ppermute(last, axis, up)
        after = lax.ppermute(first, axis, down)
        shard = jnp.concatenate([before, shard, after], axis=dim)
    return shard


def partner_offsets(tile_count, device_count):
    return [
        1,
        -1,
        2,
        -2,
        tile_count,
        -tile_count,
        tile_count + 1,
        -(tile_count + 1),
        2 * tile_count,
        -2 * tile_count,
        device_count // 2,
    ]


def time_derivative(values, derivative, jacobian, inv_density, lame_lambda, shear_modulus):
    basis_count = values.shape[0]
    quant_count = values.shape[1]
    elem_count = values.shape[2]
    flat = values.reshape(basis_count, quant_count * elem_count)
    gradient = jnp.dot(derivative.reshape(3 * basis_count, basis_count), flat, precision=highest)
    gradient = gradient.reshape(3, basis_count, quant_count, elem_count)
    physical = [
        jacobian[0, x][None, None, :] * gradient[0]
        + jacobian[1, x][None, None, :] * gradient[1]
        + jacobian[2, x][None, None, :] * gradient[2]
        for x in range(3)
    ]
    velocity_grad = [[physical[j][:, 6 + i] for j in range(3)] for i in range(3)]
    divergence = velocity_grad[0][0] + velocity_grad[1][1] + velocity_grad[2][2]

    def stress(i, j):
        mixed = shear_modulus * (velocity_grad[i][j] + velocity_grad[j][i])
        return lame_lambda * divergence + mixed if i == j else mixed

    acceleration = [
        inv_density
        * (
            physical[0][:, STRESS_PAIRS[i][0]]
            + physical[1][:, STRESS_PAIRS[i][1]]
            + physical[2][:, STRESS_PAIRS[i][2]]
        )
        for i in range(3)
    ]
    return jnp.stack(
        [stress(0, 0), stress(1, 1), stress(2, 2), stress(0, 1), stress(1, 2), stress(0, 2)]
        + acceleration,
        axis=1,
    )


def predict(dof_values, derivative, jacobian, inv_density, lame_lambda, shear_modulus):
    integral = step_size * dof_values
    taylor_term = dof_values
    factor = step_size
    for k in range(1, 4):
        taylor_term = time_derivative(
            taylor_term, derivative, jacobian, inv_density, lame_lambda, shear_modulus
        )
        factor = factor * step_size / (k + 1)
        integral = integral + factor * taylor_term
    return integral


def normal_operator(jump_value, normals, inv_density, lame_lambda, shear_modulus):
    direction = [normals[:, d, :] for d in range(3)]
    velocity_jump = [jump_value[:, 6 + d] for d in range(3)]
    normal_flow = (
        velocity_jump[0] * direction[0]
        + velocity_jump[1] * direction[1]
        + velocity_jump[2] * direction[2]
    )
    traction = [
        inv_density
        * (
            jump_value[:, STRESS_PAIRS[i][0]] * direction[0]
            + jump_value[:, STRESS_PAIRS[i][1]] * direction[1]
            + jump_value[:, STRESS_PAIRS[i][2]] * direction[2]
        )
        for i in range(3)
    ]

    def stress(i, j):
        mixed = shear_modulus * (velocity_jump[i] * direction[j] + velocity_jump[j] * direction[i])
        return lame_lambda * normal_flow + mixed if i == j else mixed

    return jnp.stack(
        [stress(0, 0), stress(1, 1), stress(2, 2), stress(0, 1), stress(1, 2), stress(0, 2)]
        + traction,
        axis=1,
    )


def shards(
    dof_values,
    density,
    lame_lambda,
    shear_modulus,
    jacobian,
    normals,
    face_scale,
    derivative,
    face_proj,
    lift_matrix,
    neighbour,
    send_face,
    cluster,
    sea_face,
    sea_cell,
    height,
    momentum,
    ocean_depth,
):
    basis_count = dof_values.shape[0]
    quant_count = dof_values.shape[1]
    elem_count = dof_values.shape[2]
    face_count = face_proj.shape[1]
    inv_density = 1.0 / density
    integral = predict(dof_values, derivative, jacobian, inv_density, lame_lambda, shear_modulus)
    projected = jnp.dot(
        face_proj.reshape(4 * face_count, basis_count),
        integral.reshape(basis_count, quant_count * elem_count),
        precision=highest,
    )
    traces = jnp.transpose(projected.reshape(4, face_count, quant_count, elem_count), (1, 2, 0, 3))
    face_table = traces.reshape(face_count * quant_count, 4 * elem_count)
    outgoing = jnp.take(face_table, send_face, axis=1)
    table_rows = outgoing.shape[0]
    partner_count = send_face.shape[0]
    slot_count = send_face.shape[1]
    device_count = lax.axis_size("dom") * lax.axis_size("tile")
    offset_list = partner_offsets(lax.axis_size("tile"), device_count)
    offsets = jnp.array(offset_list, jnp.int32)
    here = lax.axis_index(("dom", "tile"))
    target = (here + offsets) % device_count
    padded = (
        jnp.zeros((table_rows, device_count, slot_count), jnp.float32)
        .at[:, target, :]
        .set(outgoing)
    )
    received = lax.all_to_all(padded, ("dom", "tile"), split_axis=1, concat_axis=1, tiled=True)
    source = (here - offsets) % device_count
    incoming = jnp.take(received, source, axis=1)
    incoming = incoming.reshape(table_rows, partner_count * slot_count)
    upward = traces[0, 8, 0]
    handed = jnp.where(sea_face >= 0, jnp.take(upward, jnp.maximum(sea_face, 0)), 0.0)
    arrived = lax.all_to_all(handed, ("dom", "tile"), split_axis=0, concat_axis=0, tiled=True)
    uplift = (
        jnp.zeros((height.shape[0] * height.shape[1],), jnp.float32)
        .at[sea_cell.reshape(-1)]
        .add(arrived.reshape(-1))
        .reshape(height.shape)
    )
    volume = time_derivative(
        integral, derivative, jacobian, inv_density, lame_lambda, shear_modulus
    )
    lookup = jnp.concatenate([face_table, incoming], axis=1)
    neighbour_trace = jnp.take(lookup, neighbour, axis=1).reshape(traces.shape)
    jump_value = neighbour_trace - traces
    wave_speed = jnp.sqrt((lame_lambda + 2.0 * shear_modulus) * inv_density)
    correction = (
        0.5
        * face_scale
        * (
            normal_operator(jump_value, normals, inv_density, lame_lambda, shear_modulus)
            + wave_speed * jump_value
        )
    )
    correction_rows = jnp.transpose(correction, (2, 0, 1, 3)).reshape(
        4 * face_count, quant_count * elem_count
    )
    lift_rows = jnp.transpose(lift_matrix, (1, 0, 2)).reshape(basis_count, 4 * face_count)
    lifted = jnp.dot(lift_rows, correction_rows, precision=highest).reshape(
        basis_count, quant_count, elem_count
    )
    updated = dof_values + volume + lifted
    dof_out = jnp.where(cluster[None, None, :] == 1, updated, dof_values)
    level = height + uplift
    flow_x, flow_y = (momentum[0], momentum[1])
    for k in range(STEPS):
        rims = extended(jnp.stack([flow_x, flow_y]), (("dom", 1), ("tile", 2)), 1)
        spread = rims[0, 2:, 1:-1] - rims[0, :-2, 1:-1] + (rims[1, 1:-1, 2:] - rims[1, 1:-1, :-2])
        level = level - 0.5 * wave_rate * spread
        level_rim = extended(level, (("dom", 0), ("tile", 1)), 1)
        flow_x = flow_x - 0.5 * wave_rate * ocean_depth * (
            level_rim[2:, 1:-1] - level_rim[:-2, 1:-1]
        )
        flow_y = flow_y - 0.5 * wave_rate * ocean_depth * (
            level_rim[1:-1, 2:] - level_rim[1:-1, :-2]
        )
    return (dof_out, level, jnp.stack([flow_x, flow_y]))


def solution(mesh):
    return jax.shard_map(
        shards,
        mesh=mesh,
        in_specs=(
            P(None, None, ("dom", "tile")),
            P(("dom", "tile")),
            P(("dom", "tile")),
            P(("dom", "tile")),
            P(None, None, ("dom", "tile")),
            P(None, None, ("dom", "tile")),
            P(None, ("dom", "tile")),
            P(),
            P(),
            P(),
            P(None, ("dom", "tile")),
            P(("dom", "tile"), None),
            P(("dom", "tile")),
            P(("dom", "tile"), None),
            P(("dom", "tile"), None),
            P("dom", "tile"),
            P(None, "dom", "tile"),
            P("dom", "tile"),
        ),
        out_specs=(P(None, None, ("dom", "tile")), P("dom", "tile"), P(None, "dom", "tile")),
        check_vma=False,
    )
```

profile of v0, /device:TPU:25, one launch (start us, length us, event | category | flops | bytes accessed | tf_op | source)
XLA Modules:
  0.0 314.0 jit_solution(2958480596675993151)
XLA Ops:
  2.0 2.4 collective-permute-start
  4.4 5.0 %collective-permute-start.1 = (f32[2,1,512]{2,1,0:T(1,128)}, f32[2,1,512]{2,1,0:T(1,128)}, u32[]{:S(2)}, u32[]{:S(2)}) collective-permute-start(f32[2,1,512]{2,1,0:T(1,128)} %get-tuple-element.104), channel_id=1, source_target_pairs={{0,8},{8,16},{16,24},{24,32},{32,40},{40,48},{48,56},{56,64},{64,7... | collective-permute-start | bytes 12296 | tf_op jit(solution)/shard_map/ppermute | solution.py:22
  28.6 51.2 %gather_fusion.3 = f32[8192]{0:T(1024)S(1)} fusion(f32[512]{0:T(512)S(1)} %bitcast.116, s32[8192]{0:T(1024)S(1)} %broadcast_clamp_fusion), kind=kCustom, calls=%fused_computation.3 | custom fusion | bytes 98304 | tf_op jit(solution)/shard_map/jit(_take)/gather | solution.py:174
  80.6 11.2 %all-to-all-start.1 = ((f32[128,1,64]{2,1,0:T(1,128)}), f32[128,1,64]{2,1,0:T(1,128)}, u32[]{:S(2)}, u32[]{:S(2)}) async-start(f32[128,1,64]{2,1,0:T(1,128)} %bitcast.30), calls=%async_computation.1 | async-start | bytes 131072 | tf_op jit(solution)/shard_map/all_to_all | solution.py:175
  98.3 2.4 scatter_fusion
  102.1 3.4 %collective-permute-start.3 = (f32[2,66,1]{2,1,0:T(8,128)}, f32[2,66,1]{2,1,0:T(8,128)S(1)}, u32[]{:S(2)}, u32[]{:S(2)}) collective-permute-start(f32[2,66,1]{2,1,0:T(8,128)} %get-tuple-element.93), channel_id=1, source_target_pairs={{0,1},{1,2},{2,3},{3,4},{4,5},{5,6},{6,7},{8,9},{9,10},{10,11},{11... | collective-permute-start | bytes 1592 | tf_op jit(solution)/shard_map/ppermute | solution.py:22
  105.5 2.1 collective-permute-start.2
  107.6 10.5 %all-to-all-start = ((f32[90,128,32]{0,2,1:T(8,128)}), f32[90,128,32]{0,2,1:T(8,128)}, u32[]{:S(2)}, u32[]{:S(2)}) async-start(f32[90,128,32]{0,2,1:T(8,128)} %scatter_fusion), calls=%async_computation | async-start | bytes 4194304 | tf_op jit(solution)/shard_map/all_to_all | solution.py:169
  120.3 43.4 %scatter_custom_fusion.1 = f32[32768]{0:T(1024)S(1)} fusion(s32[8192]{0:T(1024)} %bitcast.183, f32[8192]{0:T(1024)S(1)} %reshape.422, f32[]{:T(128)} %constant.109.clone.1), kind=kCustom, calls=%fused_computation.195 | custom fusion | flops 8192 | bytes 131584 | tf_op jit(solution)/shard_map/scatter-add | solution.py:179
  164.8 3.2 %collective-permute-start.5 = (f32[1,512]{1,0:T(1,128)S(1)}, f32[1,512]{1,0:T(1,128)S(1)}, u32[]{:S(2)}, u32[]{:S(2)}) collective-permute-start(f32[1,512]{1,0:T(1,128)S(1)} %get-tuple-element.120), channel_id=1, source_target_pairs={{0,8},{8,16},{16,24},{24,32},{32,40},{40,48},{48,56},{56,64},{64,7... | collective-permute-start | bytes 6152 | tf_op jit(solution)/shard_map/ppermute | solution.py:22
  167.9 2.1 collective-permute-start.4
  173.5 1.9 squeeze.39
  175.5 3.9 %collective-permute-start.7 = (f32[66,1]{1,0:T(8,128)S(1)}, f32[66,1]{1,0:T(8,128)S(1)}, u32[]{:S(2)}, u32[]{:S(2)}) collective-permute-start(f32[66,1]{1,0:T(8,128)S(1)} %get-tuple-element.113), channel_id=1, source_target_pairs={{0,1},{1,2},{2,3},{3,4},{4,5},{5,6},{6,7},{8,9},{9,10},{10,11},{11... | collective-permute-start | bytes 800 | tf_op jit(solution)/shard_map/ppermute | solution.py:22
  179.4 2.1 collective-permute-start.6
  185.0 2.4 collective-permute-start.8
  187.5 5.0 %collective-permute-start.9 = (f32[2,1,512]{2,1,0:T(1,128)S(1)}, f32[2,1,512]{2,1,0:T(1,128)S(1)}, u32[]{:S(2)}, u32[]{:S(2)}) collective-permute-start(f32[2,1,512]{2,1,0:T(1,128)S(1)} %get-tuple-element.102), channel_id=1, source_target_pairs={{0,8},{8,16},{16,24},{24,32},{32,40},{40,48},{48,56},{56,64},{64,7... | collective-permute-start | bytes 12296 | tf_op jit(solution)/shard_map/ppermute | solution.py:22
  193.3 3.0 collective-permute-start.11
  196.3 1.9 collective-permute-start.10
  198.5 3.5 %collective-permute-done.10 = f32[2,66,1]{2,1,0:T(8,128)S(1)} collective-permute-done((f32[2,66,1]{2,1,0:T(8,128)S(1)}, f32[2,66,1]{2,1,0:T(8,128)S(1)}, u32[]{:S(2)}, u32[]{:S(2)}) %collective-permute-start.10) | collective-permute-done | bytes 560 | tf_op jit(solution)/shard_map/ppermute | solution.py:23
  202.2 6.0 %collective-permute-start.13 = (f32[1,512]{1,0:T(1,128)S(1)}, f32[1,512]{1,0:T(1,128)S(1)}, u32[]{:S(2)}, u32[]{:S(2)}) collective-permute-start(f32[1,512]{1,0:T(1,128)S(1)} %get-tuple-element.118), channel_id=1, source_target_pairs={{0,8},{8,16},{16,24},{24,32},{32,40},{40,48},{48,56},{56,64},{64,7... | collective-permute-start | bytes 6152 | tf_op jit(solution)/shard_map/ppermute | solution.py:22
  208.2 1.9 collective-permute-start.12
  210.2 4.5 %collective-permute-done.12 = f32[1,512]{1,0:T(1,128)S(1)} collective-permute-done((f32[1,512]{1,0:T(1,128)S(1)}, f32[1,512]{1,0:T(1,128)S(1)}, u32[]{:S(2)}, u32[]{:S(2)}) %collective-permute-start.12) | collective-permute-done | bytes 2080 | tf_op jit(solution)/shard_map/ppermute | solution.py:23
  214.7 3.3 %collective-permute-start.15 = (f32[66,1]{1,0:T(8,128)S(1)}, f32[66,1]{1,0:T(8,128)S(1)}, u32[]{:S(2)}, u32[]{:S(2)}) collective-permute-start(f32[66,1]{1,0:T(8,128)S(1)} %get-tuple-element.111), channel_id=1, source_target_pairs={{0,1},{1,2},{2,3},{3,4},{4,5},{5,6},{6,7},{8,9},{9,10},{10,11},{11... | collective-permute-start | bytes 800 | tf_op jit(solution)/shard_map/ppermute | solution.py:22
  218.0 1.9 collective-permute-start.14
  220.0 3.3 %collective-permute-done.14 = f32[66,1]{1,0:T(8,128)S(1)} collective-permute-done((f32[66,1]{1,0:T(8,128)S(1)}, f32[66,1]{1,0:T(8,128)S(1)}, u32[]{:S(2)}, u32[]{:S(2)}) %collective-permute-start.14) | collective-permute-done | bytes 296 | tf_op jit(solution)/shard_map/ppermute | solution.py:23
  223.5 1.9 collective-permute-start.16
  225.4 5.5 %collective-permute-start.17 = (f32[2,1,512]{2,1,0:T(1,128)S(1)}, f32[2,1,512]{2,1,0:T(1,128)S(1)}, u32[]{:S(2)}, u32[]{:S(2)}) collective-permute-start(f32[2,1,512]{2,1,0:T(1,128)S(1)} %get-tuple-element.100), channel_id=1, source_target_pairs={{0,8},{8,16},{16,24},{24,32},{32,40},{40,48},{48,56},{56,64},{64,7... | collective-permute-start | bytes 12296 | tf_op jit(solution)/shard_map/ppermute | solution.py:22
  231.7 3.0 collective-permute-start.19
  234.7 1.9 collective-permute-start.18
  236.7 3.7 %collective-permute-done.18 = f32[2,66,1]{2,1,0:T(8,128)S(1)} collective-permute-done((f32[2,66,1]{2,1,0:T(8,128)S(1)}, f32[2,66,1]{2,1,0:T(8,128)S(1)}, u32[]{:S(2)}, u32[]{:S(2)}) %collective-permute-start.18) | collective-permute-done | bytes 560 | tf_op jit(solution)/shard_map/ppermute | solution.py:23
  240.6 1.9 collective-permute-start.20
  242.5 6.0 %collective-permute-start.21 = (f32[1,512]{1,0:T(1,128)S(1)}, f32[1,512]{1,0:T(1,128)S(1)}, u32[]{:S(2)}, u32[]{:S(2)}) collective-permute-start(f32[1,512]{1,0:T(1,128)S(1)} %get-tuple-element.116), channel_id=1, source_target_pairs={{0,8},{8,16},{16,24},{24,32},{32,40},{40,48},{48,56},{56,64},{64,7... | collective-permute-start | bytes 6152 | tf_op jit(solution)/shard_map/ppermute | solution.py:22
  249.4 2.7 collective-permute-start.23
  252.1 1.9 collective-permute-start.22
  254.1 3.2 %collective-permute-done.22 = f32[66,1]{1,0:T(8,128)S(1)} collective-permute-done((f32[66,1]{1,0:T(8,128)S(1)}, f32[66,1]{1,0:T(8,128)S(1)}, u32[]{:S(2)}, u32[]{:S(2)}) %collective-permute-start.22) | collective-permute-done | bytes 296 | tf_op jit(solution)/shard_map/ppermute | solution.py:23
  257.6 1.9 collective-permute-start.24
  259.5 6.0 %collective-permute-start.25 = (f32[2,1,512]{2,1,0:T(1,128)S(1)}, f32[2,1,512]{2,1,0:T(1,128)S(1)}, u32[]{:S(2)}, u32[]{:S(2)}) collective-permute-start(f32[2,1,512]{2,1,0:T(1,128)S(1)} %get-tuple-element.98), channel_id=1, source_target_pairs={{0,8},{8,16},{16,24},{24,32},{32,40},{40,48},{48,56},{56,64},{64,7... | collective-permute-start | bytes 12296 | tf_op jit(solution)/shard_map/ppermute | solution.py:22
  266.4 2.8 collective-permute-start.27
  269.2 1.9 collective-permute-start.26
  271.1 3.7 %collective-permute-done.26 = f32[2,66,1]{2,1,0:T(8,128)S(1)} collective-permute-done((f32[2,66,1]{2,1,0:T(8,128)S(1)}, f32[2,66,1]{2,1,0:T(8,128)S(1)}, u32[]{:S(2)}, u32[]{:S(2)}) %collective-permute-start.26) | collective-permute-done | bytes 560 | tf_op jit(solution)/shard_map/ppermute | solution.py:23
  275.0 6.0 %collective-permute-start.29 = (f32[1,512]{1,0:T(1,128)S(1)}, f32[1,512]{1,0:T(1,128)S(1)}, u32[]{:S(2)}, u32[]{:S(2)}) collective-permute-start(f32[1,512]{1,0:T(1,128)S(1)} %get-tuple-element.114), channel_id=1, source_target_pairs={{0,8},{8,16},{16,24},{24,32},{32,40},{40,48},{48,56},{56,64},{64,7... | collective-permute-start | bytes 6152 | tf_op jit(solution)/shard_map/ppermute | solution.py:22
  281.1 1.9 collective-permute-start.28
  283.8 3.7 %collective-permute-done.28 = f32[1,512]{1,0:T(1,128)S(1)} collective-permute-done((f32[1,512]{1,0:T(1,128)S(1)}, f32[1,512]{1,0:T(1,128)S(1)}, u32[]{:S(2)}, u32[]{:S(2)}) %collective-permute-start.28) | collective-permute-done | bytes 2080 | tf_op jit(solution)/shard_map/ppermute | solution.py:23
  287.6 3.3 %collective-permute-start.31 = (f32[66,1]{1,0:T(8,128)S(1)}, f32[66,1]{1,0:T(8,128)S(1)}, u32[]{:S(2)}, u32[]{:S(2)}) collective-permute-start(f32[66,1]{1,0:T(8,128)S(1)} %get-tuple-element.107), channel_id=1, source_target_pairs={{0,1},{1,2},{2,3},{3,4},{4,5},{5,6},{6,7},{8,9},{9,10},{10,11},{11... | collective-permute-start | bytes 800 | tf_op jit(solution)/shard_map/ppermute | solution.py:22
  290.9 1.9 collective-permute-start.30
  293.7 2.4 collective-permute-done.30
  297.0 2.1 gather_fusion.1
  300.0 7.6 %gather_fusion.2 = f32[2048,90]{1,0:T(8,128)} fusion(f32[90,2400]{0,1:T(8,128)S(1)} %pad_maximum_fusion, s32[2048]{0:T(1024)S(1)} %copy-done.26), kind=kCustom, calls=%fused_computation.2 | custom fusion | bytes 1482752 | tf_op jit(solution)/shard_map/jit(_take)/gather | solution.py:186
  (248 shorter events, 52.9 us)
Async XLA Ops:
  2.0 98.7 %collective-permute-start = (f32[2,1,512]{2,1,0:T(1,128)}, f32[2,1,512]{2,1,0:T(1,128)}, u32[]{:S(2)}, u32[]{:S(2)}) collective-permute-start(f32[2,1,512]{2,1,0:T(1,128)} %get-tuple-element.105), channel_id=1, source_target_pairs={{8,0},{16,8},{24,16},{32,24},{40,32},{48,40},{56,48},{64,56},{72,6... | collective-permute-start | bytes 12296 | tf_op jit(solution)/shard_map/ppermute | solution.py:23
  4.4 96.3 %collective-permute-start.1 = (f32[2,1,512]{2,1,0:T(1,128)}, f32[2,1,512]{2,1,0:T(1,128)}, u32[]{:S(2)}, u32[]{:S(2)}) collective-permute-start(f32[2,1,512]{2,1,0:T(1,128)} %get-tuple-element.104), channel_id=1, source_target_pairs={{0,8},{8,16},{16,24},{24,32},{32,40},{40,48},{48,56},{56,64},{64,7... | collective-permute-start | bytes 12296 | tf_op jit(solution)/shard_map/ppermute | solution.py:22
  27.6 64.2 %copy-start = (f32[4,10,9,512]{3,2,1,0:T(8,128)}, f32[4,10,9,512]{3,2,1,0:T(8,128)S(1)}, u32[]{:S(2)}) copy-start(f32[4,10,9,512]{3,2,1,0:T(8,128)S(1)} %reshape.370) | copy-start | bytes 2211844
  79.9 12.5 %copy-start.29 = (s32[11,32]{1,0:T(8,128)S(1)}, s32[11,32]{1,0:T(8,128)}, u32[]{:S(2)}) copy-start(s32[11,32]{1,0:T(8,128)} %param.30) | copy-start | bytes 4228
  80.6 27.0 %all-to-all-start.1 = ((f32[128,1,64]{2,1,0:T(1,128)}), f32[128,1,64]{2,1,0:T(1,128)}, u32[]{:S(2)}, u32[]{:S(2)}) async-start(f32[128,1,64]{2,1,0:T(1,128)} %bitcast.30), calls=%async_computation.1 | async-start | bytes 131072 | tf_op jit(solution)/shard_map/all_to_all | solution.py:175
  102.1 61.6 %collective-permute-start.3 = (f32[2,66,1]{2,1,0:T(8,128)}, f32[2,66,1]{2,1,0:T(8,128)S(1)}, u32[]{:S(2)}, u32[]{:S(2)}) collective-permute-start(f32[2,66,1]{2,1,0:T(8,128)} %get-tuple-element.93), channel_id=1, source_target_pairs={{0,1},{1,2},{2,3},{3,4},{4,5},{5,6},{6,7},{8,9},{9,10},{10,11},{11... | collective-permute-start | bytes 1592 | tf_op jit(solution)/shard_map/ppermute | solution.py:22
  105.5 58.3 %copy-start.7 = (f32[64,512]{1,0:T(8,128)S(1)}, f32[64,512]{1,0:T(8,128)}, u32[]{:S(2)}) copy-start(f32[64,512]{1,0:T(8,128)} %param.34) | copy-start | bytes 393220
  105.5 58.3 %collective-permute-start.2 = (f32[2,66,1]{2,1,0:T(8,128)S(1)}, f32[2,66,1]{2,1,0:T(8,128)}, u32[]{:S(2)}, u32[]{:S(2)}) collective-permute-start(f32[2,66,1]{2,1,0:T(8,128)S(1)} %get-tuple-element.92), channel_id=1, source_target_pairs={{1,0},{2,1},{3,2},{4,3},{5,4},{6,5},{7,6},{9,8},{10,9},{11,10},{12... | collective-permute-start | bytes 1592 | tf_op jit(solution)/shard_map/ppermute | solution.py:23
  107.6 189.5 %all-to-all-start = ((f32[90,128,32]{0,2,1:T(8,128)}), f32[90,128,32]{0,2,1:T(8,128)}, u32[]{:S(2)}, u32[]{:S(2)}) async-start(f32[90,128,32]{0,2,1:T(8,128)} %scatter_fusion), calls=%async_computation | async-start | bytes 4194304 | tf_op jit(solution)/shard_map/all_to_all | solution.py:169
  164.8 10.6 %collective-permute-start.5 = (f32[1,512]{1,0:T(1,128)S(1)}, f32[1,512]{1,0:T(1,128)S(1)}, u32[]{:S(2)}, u32[]{:S(2)}) collective-permute-start(f32[1,512]{1,0:T(1,128)S(1)} %get-tuple-element.120), channel_id=1, source_target_pairs={{0,8},{8,16},{16,24},{24,32},{32,40},{40,48},{48,56},{56,64},{64,7... | collective-permute-start | bytes 6152 | tf_op jit(solution)/shard_map/ppermute | solution.py:22
  167.9 7.5 %collective-permute-start.4 = (f32[1,512]{1,0:T(1,128)S(1)}, f32[1,512]{1,0:T(1,128)S(1)}, u32[]{:S(2)}, u32[]{:S(2)}) collective-permute-start(f32[1,512]{1,0:T(1,128)S(1)} %get-tuple-element.121), channel_id=1, source_target_pairs={{8,0},{16,8},{24,16},{32,24},{40,32},{48,40},{56,48},{64,56},{72,6... | collective-permute-start | bytes 6152 | tf_op jit(solution)/shard_map/ppermute | solution.py:23
  172.3 9.2 %copy-start.11 = (f32[1,1,512]{2,1,0:T(1,128)S(1)}, f32[1,1,512]{2,1,0:T(1,128)}, u32[]{:S(2)}) copy-start(f32[1,1,512]{2,1,0:T(1,128)} %copy-done.10) | copy-start | bytes 6148
  172.3 9.2 %copy-start.13 = (f32[1,1,512]{2,1,0:T(1,128)S(1)}, f32[1,1,512]{2,1,0:T(1,128)}, u32[]{:S(2)}) copy-start(f32[1,1,512]{2,1,0:T(1,128)} %copy-done.12) | copy-start | bytes 6148
  172.3 9.2 %copy-start.15 = (f32[1,1,512]{2,1,0:T(1,128)S(1)}, f32[1,1,512]{2,1,0:T(1,128)}, u32[]{:S(2)}) copy-start(f32[1,1,512]{2,1,0:T(1,128)} %copy-done.14) | copy-start | bytes 6148
  172.3 9.2 %copy-start.17 = (f32[1,1,512]{2,1,0:T(1,128)S(1)}, f32[1,1,512]{2,1,0:T(1,128)}, u32[]{:S(2)}) copy-start(f32[1,1,512]{2,1,0:T(1,128)} %copy-done.16) | copy-start | bytes 6148
  175.5 7.5 %collective-permute-start.7 = (f32[66,1]{1,0:T(8,128)S(1)}, f32[66,1]{1,0:T(8,128)S(1)}, u32[]{:S(2)}, u32[]{:S(2)}) collective-permute-start(f32[66,1]{1,0:T(8,128)S(1)} %get-tuple-element.113), channel_id=1, source_target_pairs={{0,1},{1,2},{2,3},{3,4},{4,5},{5,6},{6,7},{8,9},{9,10},{10,11},{11... | collective-permute-start | bytes 800 | tf_op jit(solution)/shard_map/ppermute | solution.py:22
  179.4 5.4 %collective-permute-start.6 = (f32[66,1]{1,0:T(8,128)S(1)}, f32[66,1]{1,0:T(8,128)S(1)}, u32[]{:S(2)}, u32[]{:S(2)}) collective-permute-start(f32[66,1]{1,0:T(8,128)S(1)} %get-tuple-element.112), channel_id=1, source_target_pairs={{1,0},{2,1},{3,2},{4,3},{5,4},{6,5},{7,6},{9,8},{10,9},{11,10},{12... | collective-permute-start | bytes 800 | tf_op jit(solution)/shard_map/ppermute | solution.py:23
  185.0 25.1 %copy-start.31 = (f32[4,3,512]{2,0,1:T(4,128)S(1)}, f32[4,3,512]{2,0,1:T(4,128)}, u32[]{:S(2)}) copy-start(f32[4,3,512]{2,0,1:T(4,128)} %param.24) | copy-start | bytes 73732
  185.0 7.9 %collective-permute-start.8 = (f32[2,1,512]{2,1,0:T(1,128)S(1)}, f32[2,1,512]{2,1,0:T(1,128)S(1)}, u32[]{:S(2)}, u32[]{:S(2)}) collective-permute-start(f32[2,1,512]{2,1,0:T(1,128)S(1)} %get-tuple-element.103), channel_id=1, source_target_pairs={{8,0},{16,8},{24,16},{32,24},{40,32},{48,40},{56,48},{64,56},{72,6... | collective-permute-start | bytes 12296 | tf_op jit(solution)/shard_map/ppermute | solution.py:23
  187.5 5.7 %collective-permute-start.9 = (f32[2,1,512]{2,1,0:T(1,128)S(1)}, f32[2,1,512]{2,1,0:T(1,128)S(1)}, u32[]{:S(2)}, u32[]{:S(2)}) collective-permute-start(f32[2,1,512]{2,1,0:T(1,128)S(1)} %get-tuple-element.102), channel_id=1, source_target_pairs={{0,8},{8,16},{16,24},{24,32},{32,40},{40,48},{48,56},{56,64},{64,7... | collective-permute-start | bytes 12296 | tf_op jit(solution)/shard_map/ppermute | solution.py:22
  192.4 27.5 %copy-start.30 = (s32[4,512]{1,0:T(4,128)S(1)}, s32[4,512]{1,0:T(4,128)}, u32[]{:S(2)}) copy-start(s32[4,512]{1,0:T(4,128)} %param.29) | copy-start | bytes 24580
  193.3 5.2 %collective-permute-start.11 = (f32[2,66,1]{2,1,0:T(8,128)S(1)}, f32[2,66,1]{2,1,0:T(8,128)S(1)}, u32[]{:S(2)}, u32[]{:S(2)}) collective-permute-start(f32[2,66,1]{2,1,0:T(8,128)S(1)} %get-tuple-element.91), channel_id=1, source_target_pairs={{0,1},{1,2},{2,3},{3,4},{4,5},{5,6},{6,7},{8,9},{9,10},{10,11},{11... | collective-permute-start | bytes 1592 | tf_op jit(solution)/shard_map/ppermute | solution.py:22
  196.3 5.7 %collective-permute-start.10 = (f32[2,66,1]{2,1,0:T(8,128)S(1)}, f32[2,66,1]{2,1,0:T(8,128)S(1)}, u32[]{:S(2)}, u32[]{:S(2)}) collective-permute-start(f32[2,66,1]{2,1,0:T(8,128)S(1)} %get-tuple-element.90), channel_id=1, source_target_pairs={{1,0},{2,1},{3,2},{4,3},{5,4},{6,5},{7,6},{9,8},{10,9},{11,10},{12... | collective-permute-start | bytes 1592 | tf_op jit(solution)/shard_map/ppermute | solution.py:23
  198.4 38.2 %copy-start.36 = (f32[4,512]{1,0:T(4,128)S(1)}, f32[4,512]{1,0:T(4,128)}, u32[]{:S(2)}) copy-start(f32[4,512]{1,0:T(4,128)} %param.25) | copy-start | bytes 24580
  202.2 8.0 %collective-permute-start.13 = (f32[1,512]{1,0:T(1,128)S(1)}, f32[1,512]{1,0:T(1,128)S(1)}, u32[]{:S(2)}, u32[]{:S(2)}) collective-permute-start(f32[1,512]{1,0:T(1,128)S(1)} %get-tuple-element.118), channel_id=1, source_target_pairs={{0,8},{8,16},{16,24},{24,32},{32,40},{40,48},{48,56},{56,64},{64,7... | collective-permute-start | bytes 6152 | tf_op jit(solution)/shard_map/ppermute | solution.py:22
  208.2 6.4 %collective-permute-start.12 = (f32[1,512]{1,0:T(1,128)S(1)}, f32[1,512]{1,0:T(1,128)S(1)}, u32[]{:S(2)}, u32[]{:S(2)}) collective-permute-start(f32[1,512]{1,0:T(1,128)S(1)} %get-tuple-element.119), channel_id=1, source_target_pairs={{8,0},{16,8},{24,16},{32,24},{40,32},{48,40},{56,48},{64,56},{72,6... | collective-permute-start | bytes 6152 | tf_op jit(solution)/shard_map/ppermute | solution.py:23
  214.7 5.3 %collective-permute-start.15 = (f32[66,1]{1,0:T(8,128)S(1)}, f32[66,1]{1,0:T(8,128)S(1)}, u32[]{:S(2)}, u32[]{:S(2)}) collective-permute-start(f32[66,1]{1,0:T(8,128)S(1)} %get-tuple-element.111), channel_id=1, source_target_pairs={{0,1},{1,2},{2,3},{3,4},{4,5},{5,6},{6,7},{8,9},{9,10},{10,11},{11... | collective-permute-start | bytes 800 | tf_op jit(solution)/shard_map/ppermute | solution.py:22
  218.0 5.3 %collective-permute-start.14 = (f32[66,1]{1,0:T(8,128)S(1)}, f32[66,1]{1,0:T(8,128)S(1)}, u32[]{:S(2)}, u32[]{:S(2)}) collective-permute-start(f32[66,1]{1,0:T(8,128)S(1)} %get-tuple-element.110), channel_id=1, source_target_pairs={{1,0},{2,1},{3,2},{4,3},{5,4},{6,5},{7,6},{9,8},{10,9},{11,10},{12... | collective-permute-start | bytes 800 | tf_op jit(solution)/shard_map/ppermute | solution.py:23
  223.5 8.0 %collective-permute-start.16 = (f32[2,1,512]{2,1,0:T(1,128)S(1)}, f32[2,1,512]{2,1,0:T(1,128)S(1)}, u32[]{:S(2)}, u32[]{:S(2)}) collective-permute-start(f32[2,1,512]{2,1,0:T(1,128)S(1)} %get-tuple-element.101), channel_id=1, source_target_pairs={{8,0},{16,8},{24,16},{32,24},{40,32},{48,40},{56,48},{64,56},{72,6... | collective-permute-start | bytes 12296 | tf_op jit(solution)/shard_map/ppermute | solution.py:23
  225.4 6.2 %collective-permute-start.17 = (f32[2,1,512]{2,1,0:T(1,128)S(1)}, f32[2,1,512]{2,1,0:T(1,128)S(1)}, u32[]{:S(2)}, u32[]{:S(2)}) collective-permute-start(f32[2,1,512]{2,1,0:T(1,128)S(1)} %get-tuple-element.100), channel_id=1, source_target_pairs={{0,8},{8,16},{16,24},{24,32},{32,40},{40,48},{48,56},{56,64},{64,7... | collective-permute-start | bytes 12296 | tf_op jit(solution)/shard_map/ppermute | solution.py:22
  231.7 5.0 %collective-permute-start.19 = (f32[2,66,1]{2,1,0:T(8,128)S(1)}, f32[2,66,1]{2,1,0:T(8,128)S(1)}, u32[]{:S(2)}, u32[]{:S(2)}) collective-permute-start(f32[2,66,1]{2,1,0:T(8,128)S(1)} %get-tuple-element.89), channel_id=1, source_target_pairs={{0,1},{1,2},{2,3},{3,4},{4,5},{5,6},{6,7},{8,9},{9,10},{10,11},{11... | collective-permute-start | bytes 1592 | tf_op jit(solution)/shard_map/ppermute | solution.py:22
  234.7 5.7 %collective-permute-start.18 = (f32[2,66,1]{2,1,0:T(8,128)S(1)}, f32[2,66,1]{2,1,0:T(8,128)S(1)}, u32[]{:S(2)}, u32[]{:S(2)}) collective-permute-start(f32[2,66,1]{2,1,0:T(8,128)S(1)} %get-tuple-element.88), channel_id=1, source_target_pairs={{1,0},{2,1},{3,2},{4,3},{5,4},{6,5},{7,6},{9,8},{10,9},{11,10},{12... | collective-permute-start | bytes 1592 | tf_op jit(solution)/shard_map/ppermute | solution.py:23
  236.7 28.9 %copy-start.38 = (s32[512]{0:T(512)S(1)}, s32[512]{0:T(512)}, u32[]{:S(2)}) copy-start(s32[512]{0:T(512)} %param.31) | copy-start | bytes 6148
  240.6 30.5 %copy-start.40 = (s32[11]{0:T(128)S(1)}, s32[11]{0:T(128)}, u32[]{:S(2)}) copy-start(s32[11]{0:T(128)} %constant.119) | copy-start | bytes 136
  240.6 8.0 %collective-permute-start.20 = (f32[1,512]{1,0:T(1,128)S(1)}, f32[1,512]{1,0:T(1,128)S(1)}, u32[]{:S(2)}, u32[]{:S(2)}) collective-permute-start(f32[1,512]{1,0:T(1,128)S(1)} %get-tuple-element.117), channel_id=1, source_target_pairs={{8,0},{16,8},{24,16},{32,24},{40,32},{48,40},{56,48},{64,56},{72,6... | collective-permute-start | bytes 6152 | tf_op jit(solution)/shard_map/ppermute | solution.py:23
  242.5 6.7 %collective-permute-start.21 = (f32[1,512]{1,0:T(1,128)S(1)}, f32[1,512]{1,0:T(1,128)S(1)}, u32[]{:S(2)}, u32[]{:S(2)}) collective-permute-start(f32[1,512]{1,0:T(1,128)S(1)} %get-tuple-element.116), channel_id=1, source_target_pairs={{0,8},{8,16},{16,24},{24,32},{32,40},{40,48},{48,56},{56,64},{64,7... | collective-permute-start | bytes 6152 | tf_op jit(solution)/shard_map/ppermute | solution.py:22
  249.4 4.8 %collective-permute-start.23 = (f32[66,1]{1,0:T(8,128)S(1)}, f32[66,1]{1,0:T(8,128)S(1)}, u32[]{:S(2)}, u32[]{:S(2)}) collective-permute-start(f32[66,1]{1,0:T(8,128)S(1)} %get-tuple-element.109), channel_id=1, source_target_pairs={{0,1},{1,2},{2,3},{3,4},{4,5},{5,6},{6,7},{8,9},{9,10},{10,11},{11... | collective-permute-start | bytes 800 | tf_op jit(solution)/shard_map/ppermute | solution.py:22
  252.1 5.3 %collective-permute-start.22 = (f32[66,1]{1,0:T(8,128)S(1)}, f32[66,1]{1,0:T(8,128)S(1)}, u32[]{:S(2)}, u32[]{:S(2)}) collective-permute-start(f32[66,1]{1,0:T(8,128)S(1)} %get-tuple-element.108), channel_id=1, source_target_pairs={{1,0},{2,1},{3,2},{4,3},{5,4},{6,5},{7,6},{9,8},{10,9},{11,10},{12... | collective-permute-start | bytes 800 | tf_op jit(solution)/shard_map/ppermute | solution.py:23
  254.1 29.1 %copy-start.33 = (f32[4,20,10]{1,0,2:T(4,128)S(1)}, f32[4,20,10]{1,0,2:T(4,128)}, u32[]{:S(2)}) copy-start(f32[4,20,10]{1,0,2:T(4,128)} %param.28) | copy-start | bytes 9604
  257.6 8.6 %collective-permute-start.24 = (f32[2,1,512]{2,1,0:T(1,128)S(1)}, f32[2,1,512]{2,1,0:T(1,128)S(1)}, u32[]{:S(2)}, u32[]{:S(2)}) collective-permute-start(f32[2,1,512]{2,1,0:T(1,128)S(1)} %get-tuple-element.99), channel_id=1, source_target_pairs={{8,0},{16,8},{24,16},{32,24},{40,32},{48,40},{56,48},{64,56},{72,6... | collective-permute-start | bytes 12296 | tf_op jit(solution)/shard_map/ppermute | solution.py:23
  259.5 6.8 %collective-permute-start.25 = (f32[2,1,512]{2,1,0:T(1,128)S(1)}, f32[2,1,512]{2,1,0:T(1,128)S(1)}, u32[]{:S(2)}, u32[]{:S(2)}) collective-permute-start(f32[2,1,512]{2,1,0:T(1,128)S(1)} %get-tuple-element.98), channel_id=1, source_target_pairs={{0,8},{8,16},{16,24},{24,32},{32,40},{40,48},{48,56},{56,64},{64,7... | collective-permute-start | bytes 12296 | tf_op jit(solution)/shard_map/ppermute | solution.py:22
  266.4 4.7 %collective-permute-start.27 = (f32[2,66,1]{2,1,0:T(8,128)S(1)}, f32[2,66,1]{2,1,0:T(8,128)S(1)}, u32[]{:S(2)}, u32[]{:S(2)}) collective-permute-start(f32[2,66,1]{2,1,0:T(8,128)S(1)} %get-tuple-element.87), channel_id=1, source_target_pairs={{0,1},{1,2},{2,3},{3,4},{4,5},{5,6},{6,7},{8,9},{9,10},{10,11},{11... | collective-permute-start | bytes 1592 | tf_op jit(solution)/shard_map/ppermute | solution.py:22
  269.2 5.7 %collective-permute-start.26 = (f32[2,66,1]{2,1,0:T(8,128)S(1)}, f32[2,66,1]{2,1,0:T(8,128)S(1)}, u32[]{:S(2)}, u32[]{:S(2)}) collective-permute-start(f32[2,66,1]{2,1,0:T(8,128)S(1)} %get-tuple-element.86), channel_id=1, source_target_pairs={{1,0},{2,1},{3,2},{4,3},{5,4},{6,5},{7,6},{9,8},{10,9},{11,10},{12... | collective-permute-start | bytes 1592 | tf_op jit(solution)/shard_map/ppermute | solution.py:23
  275.0 22.0 %copy-start.5 = (f32[64,512]{1,0:T(8,128)}, f32[64,512]{1,0:T(8,128)S(1)}, u32[]{:S(2)}) copy-start(f32[64,512]{1,0:T(8,128)S(1)} %fusion.12) | copy-start | bytes 393220
  275.0 8.8 %collective-permute-start.29 = (f32[1,512]{1,0:T(1,128)S(1)}, f32[1,512]{1,0:T(1,128)S(1)}, u32[]{:S(2)}, u32[]{:S(2)}) collective-permute-start(f32[1,512]{1,0:T(1,128)S(1)} %get-tuple-element.114), channel_id=1, source_target_pairs={{0,8},{8,16},{16,24},{24,32},{32,40},{40,48},{48,56},{56,64},{64,7... | collective-permute-start | bytes 6152 | tf_op jit(solution)/shard_map/ppermute | solution.py:22
  281.1 6.4 %collective-permute-start.28 = (f32[1,512]{1,0:T(1,128)S(1)}, f32[1,512]{1,0:T(1,128)S(1)}, u32[]{:S(2)}, u32[]{:S(2)}) collective-permute-start(f32[1,512]{1,0:T(1,128)S(1)} %get-tuple-element.115), channel_id=1, source_target_pairs={{8,0},{16,8},{24,16},{32,24},{40,32},{48,40},{56,48},{64,56},{72,6... | collective-permute-start | bytes 6152 | tf_op jit(solution)/shard_map/ppermute | solution.py:23
  287.6 6.2 %collective-permute-start.31 = (f32[66,1]{1,0:T(8,128)S(1)}, f32[66,1]{1,0:T(8,128)S(1)}, u32[]{:S(2)}, u32[]{:S(2)}) collective-permute-start(f32[66,1]{1,0:T(8,128)S(1)} %get-tuple-element.107), channel_id=1, source_target_pairs={{0,1},{1,2},{2,3},{3,4},{4,5},{5,6},{6,7},{8,9},{9,10},{10,11},{11... | collective-permute-start | bytes 800 | tf_op jit(solution)/shard_map/ppermute | solution.py:22
  290.9 5.3 %collective-permute-start.30 = (f32[66,1]{1,0:T(8,128)S(1)}, f32[66,1]{1,0:T(8,128)S(1)}, u32[]{:S(2)}, u32[]{:S(2)}) collective-permute-start(f32[66,1]{1,0:T(8,128)S(1)} %get-tuple-element.106), channel_id=1, source_target_pairs={{1,0},{2,1},{3,2},{4,3},{5,4},{6,5},{7,6},{9,8},{10,9},{11,10},{12... | collective-permute-start | bytes 800 | tf_op jit(solution)/shard_map/ppermute | solution.py:23
  (28 other events, 92.5 us)
where the time goes:
time: 316 us; the launch traced here: 314 us
  starting transfers between devices  122 us (39%)
  local copies, waits for them, and re-layouts  91.3 us (29%)
  other arithmetic  61.7 us (20%)
  waiting for transfers between devices  31.1 us (10%)
  matrix products  5.57 us (2%)
    ppermute x16, starting transfers between devices, extended(): before = lax.ppermute(last, axis, up)  68.1 us
    gather x2, local copies, waits for them, and re-layouts, shards(): jnp.take(upward, jnp.maximum(sea_face, 0))  51.3 us
    scatter-add x1, other arithmetic, shards(): uplift = jnp.zeros((height.shape[0] * height.shape[1],), jnp.float32).at[...  43.4 us
    ppermute x16, starting transfers between devices, extended(): after = lax.ppermute(first, axis, down)  32.1 us
    ppermute x16, waiting for transfers between devices, extended(): after = lax.ppermute(first, axis, down)  29.9 us
    all_to_all x1, starting transfers between devices, shards(): lax.all_to_all(handed, ('dom', 'tile'), split_axis=0, concat_axis=0, tile...  11.2 us
    all_to_all x1, starting transfers between devices, shards(): lax.all_to_all(padded, ('dom', 'tile'), split_axis=1, concat_axis=1, tile...  10.5 us
    gather x2, local copies, waits for them, and re-layouts, shards(): neighbour_trace = jnp.take(lookup, neighbour, axis=1).reshape(traces.shape)  9.41 us
  transfers between devices with their start and end apart: 34, of which 13 were waited for; matrix products, arithmetic and copies ran while one was open for 44% of the time, Pallas kernels for 0%

commit v1 on v0

v1 whole, which is shorter than its diff:
```python
import functools

import jax
import jax.numpy as jnp
from jax import lax
from jax.experimental import pallas as pl
from jax.experimental.pallas import tpu as pltpu
from jax.sharding import PartitionSpec as P

STEPS = 4
STRESS_PAIRS = ((0, 3, 5), (3, 1, 4), (5, 4, 2))
STRESS_ORDER = ((0, 0), (1, 1), (2, 2), (0, 1), (1, 2), (0, 2))
STEP_SIZE = 0.3
WAVE_RATE = 0.45
MESH = pl.DeviceIdType.MESH
F32 = jnp.float32
BF16 = jnp.bfloat16

B = 20
BP = 24
Q = 9
E = 512
CH = 256
LANES = 128
TILES = 16
RTILES = 3
SLOTS = 32
ROW0 = 16
ROWS = 96


def partner_offsets(tile_count, device_count):
    t = tile_count
    return [1, -1, 2, -2, t, -t, t + 1, -(t + 1), 2 * t, -2 * t, device_count // 2]


def split(x):
    high = x.astype(BF16).astype(F32)
    return high, x - high


def stacked(x):
    high, low = split(x)
    pad = jnp.zeros((8,) + x.shape[1:], F32)
    parts = [high, low, high]
    if (3 * x.shape[0]) % 16:
        parts.append(pad)
    return jnp.concatenate(parts, axis=0).astype(BF16)


def kernel(
    n_dom,
    n_tile,
    dof,
    density,
    lame,
    shear,
    jac,
    nrm,
    fscale,
    deriv,
    fproj,
    lift,
    nbr,
    send,
    cluster,
    sea_face,
    sea_cell,
    height,
    momentum,
    depth,
    dof_out,
    height_out,
    momentum_out,
    x_ref,
    base,
    out,
    tab,
    tab2,
    otail,
    acc,
    amat,
    lmat,
    sidx,
    nbr8,
    coef,
    msg,
    msg_in,
    tails,
    hand,
    hand_in,
    flow,
    flow_l,
    flow_r,
    level,
    level_l,
    level_r,
    local_sem,
    send_sem,
    recv_sem,
):
    devices = n_dom * n_tile
    dom, tile = lax.axis_index("dom"), lax.axis_index("tile")
    me = dom * n_tile + tile
    offsets = partner_offsets(n_tile, devices)
    greet = offsets + [n_tile - 1, -(n_tile - 1)]

    def device(offset):
        target = lax.rem(me + (offset + devices), devices)
        return (target // n_tile, lax.rem(target, n_tile))

    barrier = pltpu.get_barrier_semaphore()
    for o in greet:
        pl.semaphore_signal(barrier, inc=1, device_id=device(o), device_id_type=MESH)

    x_copy = pltpu.make_async_copy(dof, x_ref, local_sem.at[0])
    x_copy.start()
    grid_copies = []
    for t in range(4):
        lanes = slice(t * LANES, (t + 1) * LANES)
        rows = slice(ROW0, ROW0 + 64)
        grid_copies += [
            pltpu.make_async_copy(
                momentum.at[:, :, lanes], flow.at[0:2, t, rows, :], local_sem.at[1 + t]
            ),
            pltpu.make_async_copy(depth.at[:, lanes], flow.at[2, t, rows, :], local_sem.at[5 + t]),
            pltpu.make_async_copy(height.at[:, lanes], level.at[t, rows, :], local_sem.at[9 + t]),
        ]
    for c in grid_copies:
        c.start()

    lane = lax.broadcasted_iota(jnp.int32, (8, LANES), 1)
    sub = lax.broadcasted_iota(jnp.int32, (8, LANES), 0)

    amat[...] = jnp.zeros_like(amat)
    lmat[...] = jnp.zeros_like(lmat)
    for d in range(3):
        amat[d * BP : d * BP + B, 0:B] = deriv[d]
    for f in range(4):
        for c in range(10):
            row = fproj[c, f : f + 1, :]
            lrow = lift[c, f : f + 1, :]
            if c < 8:
                amat[72 + f * 8 + c : 73 + f * 8 + c, 0:B] = row
                lmat[f * 8 + c : f * 8 + c + 1, 0:B] = lrow
            else:
                k = 32 + f * 2 + c - 8
                amat[72 + k : 73 + k, 0:B] = row
                lmat[k : k + 1, 0:B] = lrow
                for r in range(4):
                    k = 112 + f * 8 + r * 2 + c - 8
                    amat[k : k + 1, 0:B] = row
    a_high, a_low = split(amat[...])
    a_all = a_high + pltpu.roll(a_high, BP, 1) + pltpu.roll(a_low, 2 * BP, 1)
    a_all = a_all.astype(BF16)[:, 0:80]
    l_high, l_low = split(jnp.transpose(lmat[...]))
    l_high, l_low = l_high[0:BP], l_low[0:BP]
    l_all = l_high + pltpu.roll(l_high, 40, 1) + pltpu.roll(l_low, 80, 1)
    l_all = l_all.astype(BF16)[:, 0:120]

    inv_den = 1.0 / density[...]
    speed = jnp.sqrt((lame[...] + 2.0 * shear[...]) * inv_den)
    half = 0.5 * fscale[...]
    scaled = [half * nrm[j] for j in range(3)]
    coefs = (
        scaled
        + [shear[...] * s for s in scaled]
        + [inv_den * s for s in scaled]
        + [half * speed]
    )
    for k, c in enumerate(coefs):
        for f in range(4):
            coef[k, 2 * f : 2 * f + 2, :] = jnp.broadcast_to(c[f : f + 1, :], (2, E))
    for f in range(4):
        nbr8[2 * f : 2 * f + 2, :] = jnp.broadcast_to(nbr[f : f + 1, :], (2, E))
    sidx[...] = jnp.zeros_like(sidx)
    sidx[0:11, 0:SLOTS] = send[...]

    x_copy.wait()

    def predictor(i, _):
        off = pl.multiple_of(i * CH, CH)
        cut = pl.ds(off, CH)
        rho = 1.0 / density[:, cut]
        lam = lame[:, cut]
        mu = shear[:, cut]
        mu2 = mu + mu
        jc = [[jac[d, x : x + 1, cut] for x in range(3)] for d in range(3)]

        def combine(g):
            def phys(x, v):
                return (
                    jc[0][x] * g[0:BP, v * CH : (v + 1) * CH]
                    + jc[1][x] * g[BP : 2 * BP, v * CH : (v + 1) * CH]
                    + jc[2][x] * g[2 * BP : 3 * BP, v * CH : (v + 1) * CH]
                )

            vg = [[phys(j, 6 + i) for j in range(3)] for i in range(3)]
            div = lam * (vg[0][0] + vg[1][1] + vg[2][2])
            res = [div + mu2 * vg[i][i] for i in range(3)]
            res += [mu * (vg[i][j] + vg[j][i]) for i, j in STRESS_ORDER[3:]]
            for i in range(3):
                s = STRESS_PAIRS[i]
                res.append(rho * (phys(0, s[0]) + phys(1, s[1]) + phys(2, s[2])))
            return res

        pad = jnp.zeros((BP - B, CH), F32)
        start = [jnp.concatenate([x_ref[v, :, cut], pad], axis=0) for v in range(Q)]
        term = start
        integral = [STEP_SIZE * w for w in term]
        factor = STEP_SIZE
        for k in range(1, 4):
            right = stacked(jnp.concatenate(term, axis=1))
            term = combine(jnp.dot(a_all[0:72], right, preferred_element_type=F32))
            factor = factor * STEP_SIZE / (k + 1)
            integral = [s + factor * w for s, w in zip(integral, term)]
        right = stacked(jnp.concatenate(integral, axis=1))
        g = jnp.dot(a_all, right, preferred_element_type=F32)
        volume = combine(g)
        for v in range(Q):
            cols = slice(v * CH, (v + 1) * CH)
            base[v, :, cut] = start[v] + volume[v]
            for f in range(4):
                here = pl.ds(pl.multiple_of(f * E + off, LANES), CH)
                tab[v, :, here] = g[72 + f * 8 : 80 + f * 8, cols]
                tab[Q + v, :, here] = g[112 + f * 8 : 120 + f * 8, cols]
            otail[v, :, cut] = g[104:112, cols]
        for f in range(4):
            here = pl.ds(pl.multiple_of(f * E + off, LANES), CH)
            pair = lax.broadcasted_iota(jnp.int32, (8, CH), 0) // 2
            for j in range(3):
                packed = g[112 + f * 8 : 120 + f * 8, 4 * j * CH : (4 * j + 1) * CH]
                for q in range(1, 4):
                    if 4 * j + q < Q:
                        v = 4 * j + q
                        more = g[112 + f * 8 : 120 + f * 8, v * CH : (v + 1) * CH]
                        packed = jnp.where(pair == q, more, packed)
                tab2[j, :, here] = packed
        return 0

    lax.fori_loop(0, E // CH, predictor, 0)

    shift = lax.rem(devices - me, devices)
    ups = [jnp.broadcast_to(tab[8, 0:1, t * LANES : (t + 1) * LANES], (8, LANES)) for t in range(4)]
    slots = []
    for r in range(8):
        idx = sea_face[r * 8 : r * 8 + 8, :]
        at, which = idx & (LANES - 1), idx >> 7
        val = jnp.zeros((8, LANES), F32)
        for t in range(4):
            val = jnp.where(which == t, jnp.take_along_axis(ups[t], at, axis=1), val)
        slots.append(val)
    handed = pltpu.roll(jnp.concatenate(slots, axis=0), shift, 1)
    zeros64 = jnp.zeros((64, LANES), F32)
    hand[...] = jnp.transpose(jnp.concatenate([handed, zeros64], axis=0))

    pl.semaphore_wait(barrier, len(greet))

    copies = []

    def push(src, dst, offset):
        k = len(copies)
        copy = pltpu.make_async_remote_copy(
            src_ref=src,
            dst_ref=dst,
            send_sem=send_sem.at[k],
            recv_sem=recv_sem.at[k],
            device_id=device(offset),
            device_id_type=MESH,
        )
        copy.start()
        copies.append(copy)
        return copy

    hand_offsets = (1, n_tile, devices // 2)
    hand_copies = []
    for k, o in enumerate(hand_offsets):
        row = o // 8 * 8
        hand_copies.append(push(hand.at[row : row + 8, :], hand_in.at[k], o))

    def gather(sources, idx, tiles, start):
        at, which = idx & (LANES - 1), idx >> 7
        res = list(start)
        for t in tiles:
            mask = which == t
            for k, source in enumerate(sources):
                val = jnp.take_along_axis(source[:, t * LANES : (t + 1) * LANES], at, axis=1)
                res[k] = val if res[k] is None else jnp.where(mask, val, res[k])
        return res

    block = lane // SLOTS
    places = [(v // 4, v % 4) for v in range(Q)] + [(2, 1 + j) for j in range(3)]
    dg_copies = []
    for p in range(RTILES):
        members = [n for n in range(4 * p, 4 * p + 4) if n < len(offsets)]
        idx = jnp.zeros((8, LANES), jnp.int32)
        for n in members:
            row = jnp.broadcast_to(sidx[n : n + 1, :], (8, LANES))
            idx = jnp.where(block == n % 4, pltpu.roll(row, SLOTS * (n % 4), 1), idx)
        sources = [tab.at[v] for v in range(Q)] + [tab2.at[j] for j in range(3)]
        got = gather(sources, idx, range(TILES), [None] * 12)
        for n in members:
            for r in range(3):
                packed = None
                for k, (pr, pb) in enumerate(places):
                    if pr != r:
                        continue
                    turn = (SLOTS * (pb - n % 4)) % LANES
                    val = pltpu.roll(got[k], turn, 1) if turn else got[k]
                    packed = val if packed is None else jnp.where(block == pb, val, packed)
                msg[n, r * 8 : r * 8 + 8, :] = packed
        for n in members:
            dg_copies.append(push(msg.at[n], msg_in.at[n], offsets[n]))

    for c in grid_copies:
        c.wait()

    def halos(ring, left, right):
        lead = (slice(None),) * (len(ring.shape) - 3)
        top, low = slice(ROW0, ROW0 + 8), slice(ROW0 + 56, ROW0 + 64)
        above, below = slice(ROW0 - 8, ROW0), slice(ROW0 + 64, ROW0 + 72)
        body = slice(ROW0, ROW0 + 64)
        cols = slice(0, 4)
        res = []
        for offset, src, dst in (
            (-n_tile, ring.at[lead + (cols, top)], ring.at[lead + (cols, below)]),
            (n_tile, ring.at[lead + (cols, low)], ring.at[lead + (cols, above)]),
            (-1, ring.at[lead + (0, body)], right.at[lead + (body,)]),
            (1, ring.at[lead + (3, body)], left.at[lead + (body,)]),
            (-n_tile - 1, ring.at[lead + (0, top)], right.at[lead + (below,)]),
            (-n_tile + 1, ring.at[lead + (3, top)], left.at[lead + (below,)]),
            (n_tile - 1, ring.at[lead + (0, low)], right.at[lead + (above,)]),
            (n_tile + 1, ring.at[lead + (3, low)], left.at[lead + (above,)]),
        ):
            res.append(push(src, dst, offset))
        return res

    flow_copies = halos(flow, flow_l, flow_r)

    def local_gather(et, _):
        off = pl.multiple_of(et * LANES, LANES)
        for f in range(4):
            idx = jnp.broadcast_to(nbr8[2 * f : 2 * f + 1, pl.ds(off, LANES)], (8, LANES))
            got = gather([tab.at[v] for v in range(Q)], idx, range(TILES), [None] * Q)
            for v in range(Q):
                acc[v, :, pl.ds(pl.multiple_of(f * E + off, LANES), LANES)] = got[v]
        idx = nbr8[:, pl.ds(off, LANES)]
        got = gather([tab.at[Q + v] for v in range(Q)], idx, range(TILES), [None] * Q)
        for v in range(Q):
            acc[v, :, pl.ds(pl.multiple_of(4 * E + off, LANES), LANES)] = got[v]
        return 0

    lax.fori_loop(0, 2, local_gather, 0)

    for c in hand_copies:
        c.wait_recv()
    back = (0, devices - 1, devices - n_tile, devices // 2)
    cells = pltpu.roll(sea_cell[...], shift, 1)
    cells_t = jnp.transpose(
        jnp.concatenate([cells, jnp.zeros((64, LANES), jnp.int32)], axis=0).astype(F32)
    ).astype(jnp.int32)
    values = [hand[0:1, :]]
    for k, o in enumerate(hand_offsets):
        values.append(hand_in[k, o % 8 : o % 8 + 1, :])
    row_ids = lax.broadcasted_iota(jnp.int32, (64, LANES), 0)
    highs, lows = [], []
    for k in range(0, 4, 2):
        pair_v = values[k] + pltpu.roll(values[k + 1], 64, 1)
        pair_c = cells_t[back[k] : back[k] + 1, :] + pltpu.roll(
            cells_t[back[k + 1] : back[k + 1] + 1, :], 64, 1
        )
        v_high, v_low = split(pair_v)
        here = row_ids == jnp.broadcast_to(pair_c >> 9, (64, LANES))
        highs.append(jnp.where(here, v_high, 0.0))
        lows.append(jnp.where(here, v_low, 0.0))
    left = jnp.concatenate(
        [jnp.concatenate(highs, axis=1), jnp.concatenate(lows, axis=1)], axis=0
    ).astype(BF16)
    col_ids = lax.broadcasted_iota(jnp.int32, (64, E), 1)
    picks = []
    for k in range(4):
        column = jnp.broadcast_to(cells[:, back[k] : back[k] + 1] & (E - 1), (64, E))
        picks.append(jnp.where(col_ids == column, 1.0, 0.0).astype(BF16))
    lifted = jnp.dot(left, jnp.concatenate(picks, axis=0), preferred_element_type=F32)
    for t in range(4):
        lanes = slice(t * LANES, (t + 1) * LANES)
        level[t, ROW0 : ROW0 + 64, :] += lifted[0:64, lanes] + lifted[64:128, lanes]
    level_copies = halos(level, level_l, level_r)

    lax.fori_loop(2, 4, local_gather, 0)

    for c in flow_copies:
        c.wait()
    above_ok = jnp.where(dom > 0, 1.0, 0.0)
    below_ok = jnp.where(dom < n_dom - 1, 1.0, 0.0)
    right_ok = jnp.where(tile < n_tile - 1, 1.0, 0.0)
    left_ok = jnp.where(tile > 0, 1.0, 0.0)
    span = slice(ROW0 - 8, ROW0 + 72)
    lane80 = lax.broadcasted_iota(jnp.int32, (80, LANES), 1)
    row80 = lax.broadcasted_iota(jnp.int32, (80, LANES), 0)
    row_ok = jnp.where(row80 < 8, above_ok, jnp.where(row80 >= 72, below_ok, 1.0))
    side_ok = row_ok * jnp.where(lane80 < 64, right_ok, left_ok)

    def close(ring, left, right, scale):
        for t in range(4):
            ring[t, ROW0 - 8 : ROW0, :] = ring[t, ROW0 - 8 : ROW0, :] * above_ok
            ring[t, ROW0 + 64 : ROW0 + 72, :] = ring[t, ROW0 + 64 : ROW0 + 72, :] * below_ok
        ring[4, span, :] = jnp.where(lane80 < 64, right[span, :], left[span, :]) * side_ok
        if scale is not None:
            for t in range(5):
                ring[t, span, :] = ring[t, span, :] * scale

    c0 = 0.5 * WAVE_RATE
    for k in range(3):
        close(flow.at[k], flow_l.at[k], flow_r.at[k], c0 if k == 2 else None)
    for c in level_copies:
        c.wait()
    close(level, level_l, level_r, None)
    for ring in (flow.at[0], level):
        for t in range(5):
            ring[t, 0:8, :] = jnp.zeros((8, LANES), F32)
            ring[t, ROWS - 8 : ROWS, :] = jnp.zeros((8, LANES), F32)
    up, down = slice(ROW0 - 9, ROW0 + 71), slice(ROW0 - 7, ROW0 + 73)

    def across(ring):
        vals = [ring[t, span, :] for t in range(5)]
        fwd = [pltpu.roll(x, LANES - 1, 1) for x in vals]
        bwd = [pltpu.roll(x, 1, 1) for x in vals]
        res = []
        for t in range(5):
            nxt = jnp.where(lane80 == LANES - 1, fwd[(t + 1) % 5], fwd[t])
            prv = jnp.where(lane80 == 0, bwd[(t + 4) % 5], bwd[t])
            res.append(nxt - prv)
        return res

    def wave(_, carry):
        diff = across(flow.at[1])
        for t in range(5):
            spread = (flow[0, t, down, :] - flow[0, t, up, :]) + diff[t]
            ok = side_ok if t == 4 else row_ok
            level[t, span, :] = level[t, span, :] - (c0 * ok) * spread
        diff = across(level)
        for t in range(5):
            g = flow[2, t, span, :]
            flow[0, t, span, :] = flow[0, t, span, :] - g * (level[t, down, :] - level[t, up, :])
            flow[1, t, span, :] = flow[1, t, span, :] - g * diff[t]
        return carry

    lax.fori_loop(0, STEPS, wave, 0)
    out_copies = []
    for t in range(4):
        lanes = slice(t * LANES, (t + 1) * LANES)
        rows = slice(ROW0, ROW0 + 64)
        out_copies += [
            pltpu.make_async_copy(
                flow.at[0:2, t, rows, :], momentum_out.at[:, :, lanes], local_sem.at[1 + t]
            ),
            pltpu.make_async_copy(
                level.at[t, rows, :], height_out.at[:, lanes], local_sem.at[9 + t]
            ),
        ]
    for c in out_copies:
        c.start()

    for c in dg_copies:
        c.wait_recv()
    for p in range(RTILES):
        members = [n for n in range(4 * p, 4 * p + 4) if n < len(offsets)]
        cols = slice((TILES + p) * LANES, (TILES + p + 1) * LANES)
        for k, (pr, pb) in enumerate(places):
            res = None
            for n in members:
                val = msg_in[n, pr * 8 : pr * 8 + 8, :]
                turn = (SLOTS * (n % 4 - pb)) % LANES
                val = pltpu.roll(val, turn, 1) if turn else val
                res = val if res is None else jnp.where(block == n % 4, val, res)
            if k < Q:
                tab[k, :, cols] = res
            else:
                tails[p * 3 + k - Q] = res
        for v in range(Q):
            r = 2 * (v % 4)
            first = jnp.broadcast_to(tails[p * 3 + v // 4, r : r + 1, :], (8, LANES))
            second = jnp.broadcast_to(tails[p * 3 + v // 4, r + 1 : r + 2, :], (8, LANES))
            tab[Q + v, :, cols] = jnp.where(sub % 2 == 0, first, second)

    def finish(et, _):
        off = pl.multiple_of(et * LANES, LANES)
        cut = pl.ds(off, LANES)
        lam = lame[:, cut]
        remote = range(TILES, TILES + RTILES)
        parts = [[] for _ in range(Q)]
        for f in range(5):
            here = pl.ds(pl.multiple_of(f * E + off, LANES), LANES)
            start = [acc[v, :, here] for v in range(Q)]
            if f < 4:
                idx = jnp.broadcast_to(nbr8[2 * f : 2 * f + 1, cut], (8, LANES))
                sources = [tab.at[v] for v in range(Q)]
                own = [tab[v, :, here] for v in range(Q)]
                c = [coef[k, 2 * f : 2 * f + 1, cut] for k in range(10)]
            else:
                idx = nbr8[:, cut]
                sources = [tab.at[Q + v] for v in range(Q)]
                own = [otail[v, :, cut] for v in range(Q)]
                c = [coef[k, :, cut] for k in range(10)]
            got = gather(sources, idx, remote, start)
            jump = [a - b for a, b in zip(got, own)]
            u = jump[6:9]
            n, mun, rhn, ws = c[0:3], c[3:6], c[6:9], c[9]
            flux = lam * (u[0] * n[0] + u[1] * n[1] + u[2] * n[2])
            res = []
            for i in range(3):
                push_i = u[i] * mun[i]
                res.append(flux + (push_i + push_i) + ws * jump[i])
            for k, (i, j) in enumerate(STRESS_ORDER[3:]):
                res.append(u[i] * mun[j] + u[j] * mun[i] + ws * jump[3 + k])
            for i in range(3):
                s = STRESS_PAIRS[i]
                res.append(
                    jump[s[0]] * rhn[0] + jump[s[1]] * rhn[1] + jump[s[2]] * rhn[2] + ws * u[i]
                )
            for v in range(Q):
                parts[v].append(res[v])
        right = jnp.concatenate([jnp.concatenate(x, axis=0) for x in parts], axis=1)
        high, low = split(right)
        right = jnp.concatenate([high, low, high], axis=0).astype(BF16)
        lifts = jnp.dot(l_all, right, preferred_element_type=F32)
        chosen = jnp.broadcast_to(cluster[:, cut], (B, LANES)) == 1
        for v in range(Q):
            new = base[v, 0:B, cut] + lifts[0:B, v * LANES : (v + 1) * LANES]
            out[v, :, cut] = jnp.where(chosen, new, x_ref[v, :, cut])
        return 0

    lax.fori_loop(0, E // LANES, finish, 0)
    done = pltpu.make_async_copy(out, dof_out, local_sem.at[0])
    done.start()
    for c in hand_copies + dg_copies:
        c.wait_send()
    for c in out_copies:
        c.wait()
    done.wait()


def shards(
    dof_values,
    density,
    lame_lambda,
    shear_modulus,
    jacobian,
    normals,
    face_scale,
    derivative,
    face_proj,
    lift_matrix,
    neighbour,
    send_face,
    cluster,
    sea_face,
    sea_cell,
    height,
    momentum,
    ocean_depth,
):
    n_dom, n_tile = lax.axis_size("dom"), lax.axis_size("tile")
    row = lambda x: x.reshape(1, x.shape[0])
    vmem = pl.BlockSpec(memory_space=pltpu.VMEM)
    far = pl.BlockSpec(memory_space=pl.ANY)
    table = (TILES + RTILES) * LANES
    dof_out, height_out, momentum_out = pl.pallas_call(
        functools.partial(kernel, n_dom, n_tile),
        out_shape=(
            jax.ShapeDtypeStruct((Q, B, E), F32),
            jax.ShapeDtypeStruct(height.shape, F32),
            jax.ShapeDtypeStruct(momentum.shape, F32),
        ),
        in_specs=[far] + [vmem] * 14 + [far] * 3,
        out_specs=(far, far, far),
        scratch_shapes=[
            pltpu.VMEM((Q, B, E), F32),
            pltpu.VMEM((Q, BP, E), F32),
            pltpu.VMEM((Q, B, E), F32),
            pltpu.VMEM((2 * Q, 8, table), F32),
            pltpu.VMEM((3, 8, TILES * LANES), F32),
            pltpu.VMEM((Q, 8, E), F32),
            pltpu.VMEM((Q, 8, 5 * E), F32),
            pltpu.VMEM((144, LANES), F32),
            pltpu.VMEM((LANES, LANES), F32),
            pltpu.VMEM((16, LANES), jnp.int32),
            pltpu.VMEM((8, E), jnp.int32),
            pltpu.VMEM((10, 8, E), F32),
            pltpu.VMEM((11, 24, LANES), F32),
            pltpu.VMEM((11, 24, LANES), F32),
            pltpu.VMEM((9, 8, LANES), F32),
            pltpu.VMEM((LANES, LANES), F32),
            pltpu.VMEM((3, 8, LANES), F32),
            pltpu.VMEM((3, 5, ROWS, LANES), F32),
            pltpu.VMEM((3, ROWS, LANES), F32),
            pltpu.VMEM((3, ROWS, LANES), F32),
            pltpu.VMEM((5, ROWS, LANES), F32),
            pltpu.VMEM((ROWS, LANES), F32),
            pltpu.VMEM((ROWS, LANES), F32),
            pltpu.SemaphoreType.DMA((13,)),
            pltpu.SemaphoreType.DMA((30,)),
            pltpu.SemaphoreType.DMA((30,)),
        ],
        compiler_params=pltpu.CompilerParams(collective_id=0, has_side_effects=True),
    )(
        jnp.transpose(dof_values, (1, 0, 2)),
        row(density),
        row(lame_lambda),
        row(shear_modulus),
        jacobian,
        jnp.transpose(normals, (1, 0, 2)),
        face_scale,
        derivative,
        jnp.transpose(face_proj, (1, 0, 2)),
        jnp.transpose(lift_matrix, (2, 0, 1)),
        neighbour,
        send_face,
        row(cluster),
        jnp.transpose(sea_face),
        jnp.transpose(sea_cell),
        height,
        momentum,
        ocean_depth,
    )
    return jnp.transpose(dof_out, (1, 0, 2)), height_out, momentum_out


def solution(mesh):
    both = ("dom", "tile")
    return jax.shard_map(
        shards,
        mesh=mesh,
        in_specs=(
            P(None, None, both),
            P(both),
            P(both),
            P(both),
            P(None, None, both),
            P(None, None, both),
            P(None, both),
            P(),
            P(),
            P(),
            P(None, both),
            P(both, None),
            P(both),
            P(both, None),
            P(both, None),
            P("dom", "tile"),
            P(None, "dom", "tile"),
            P("dom", "tile"),
        ),
        out_specs=(P(None, None, both), P("dom", "tile"), P(None, "dom", "tile")),
        check_vma=False,
    )
```

time: 316 us -> 28.7 us (0.09)
  the two profiles are of different devices: /device:TPU:25 before, /device:TPU:1 now
where the time goes in v1:
time: 28.7 us; the launch traced here: 28.4 us
  Pallas kernels  24.2 us (84%)
  local copies, waits for them, and re-layouts  3.54 us (12%)
  between operations  0.66 us (2%)
    pallas_call x1, Pallas kernels, shards(): pl.pallas_call(functools.partial(kernel, n_dom, n_tile), out_shape=(jax.S...  24.2 us
    unnamed x7, local copies, waits for them, and re-layouts  3.54 us

profile of v1, /device:TPU:1, one launch (start us, length us, event | category | flops | bytes accessed | tf_op | source)
XLA Modules:
  0.0 28.4 jit_solution(1684452657878765361)
XLA Ops:
  0.6 24.2 %shard_map.193 = (f32[9,20,512]{2,1,0:T(8,128)}, f32[64,512]{1,0:T(8,128)}, f32[2,64,512]{2,1,0:T(8,128)}) custom-call(f32[9,20,512]{2,1,0:T(8,128)} %bitcast.11, f32[1,512]{1,0:T(1,128)} %bitcast.18, f32[1,512]{1,0:T(1,128)} %bitcast.19, f32[1,512]{1,0:T(1,128)} %bitcast.20, f32[3,3,512]{2,1,0:T(4,128)} %jac.1, f32[3,4,512]{2,1,0:T(4,128)} %bitcast.15, ...), custom_call_target="tpu_custom_call" | custom-call | tf_op jit(solution)/shard_map/pallas_call | solution.py:569
  24.9 0.0 copy-start.1
  24.9 1.8 %copy.24 = f32[20,9,512]{2,0,1:T(8,128)} copy(f32[20,9,512]{2,0,1:T(8,128)} %bitcast.12) | data formatting | bytes 737280
  26.7 0.0 copy-done.1
  26.7 0.0 copy-start
  26.7 0.7 %copy.25 = f32[64,512]{1,0:T(8,128)} copy(f32[64,512]{1,0:T(8,128)S(1)} %copy-done.1) | data formatting | bytes 262144
  27.4 0.3 %copy-done = f32[2,64,512]{2,1,0:T(8,128)S(1)} copy-done((f32[2,64,512]{2,1,0:T(8,128)S(1)}, f32[2,64,512]{2,1,0:T(8,128)}, u32[]{:S(2)}) %copy-start) | copy-done | bytes 262168
  27.7 0.7 %copy.26 = f32[2,64,512]{2,1,0:T(8,128)} copy(f32[2,64,512]{2,1,0:T(8,128)S(1)} %copy-done) | data formatting | bytes 524288
Async XLA Ops:
  24.9 1.9 %copy-start.1 = (f32[64,512]{1,0:T(8,128)S(1)}, f32[64,512]{1,0:T(8,128)}, u32[]{:S(2)}) copy-start(f32[64,512]{1,0:T(8,128)} %get-tuple-element.13) | copy-start | bytes 393220
  26.7 1.0 %copy-start = (f32[2,64,512]{2,1,0:T(8,128)S(1)}, f32[2,64,512]{2,1,0:T(8,128)}, u32[]{:S(2)}) copy-start(f32[2,64,512]{2,1,0:T(8,128)} %get-tuple-element.14) | copy-start | bytes 786436

commit v2 on v1

--- a/solution.py
+++ b/solution.py
@@ -12,7 +12,7 @@
 STRESS_ORDER = ((0, 0), (1, 1), (2, 2), (0, 1), (1, 2), (0, 2))
 STEP_SIZE = 0.3
 WAVE_RATE = 0.45
-MESH = pl.DeviceIdType.MESH
+FLAT = pl.DeviceIdType.LOGICAL
 F32 = jnp.float32
 BF16 = jnp.bfloat16
 
@@ -22,6 +22,7 @@
 E = 512
 CH = 256
 LANES = 128
+VMEM = 58 << 20
 TILES = 16
 RTILES = 3
 SLOTS = 32
@@ -48,57 +49,74 @@
     return jnp.concatenate(parts, axis=0).astype(BF16)
 
 
-def kernel(
-    n_dom,
-    n_tile,
-    dof,
-    density,
-    lame,
-    shear,
-    jac,
-    nrm,
-    fscale,
-    deriv,
-    fproj,
-    lift,
-    nbr,
-    send,
-    cluster,
-    sea_face,
-    sea_cell,
-    height,
-    momentum,
-    depth,
-    dof_out,
-    height_out,
-    momentum_out,
-    x_ref,
-    base,
-    out,
-    tab,
-    tab2,
-    otail,
-    acc,
-    amat,
-    lmat,
-    sidx,
-    nbr8,
-    coef,
-    msg,
-    msg_in,
-    tails,
-    hand,
-    hand_in,
-    flow,
-    flow_l,
-    flow_r,
-    level,
-    level_l,
-    level_r,
-    local_sem,
-    send_sem,
-    recv_sem,
-):
+def kernel(n_dom, n_tile, *refs):
+    (
+        dof_in,
+        density_in,
+        lame_in,
+        shear_in,
+        jac_in,
+        nrm_in,
+        fscale_in,
+        deriv_in,
+        fproj_in,
+        lift_in,
+        nbr_in,
+        send_in,
+        cluster_in,
+        sea_face_in,
+        sea_cell_in,
+        height,
+        momentum,
+        depth,
+    ) = refs[:18]
+    out, flow_out, level_out = refs[18:21]
+    (
+        x_ref,
+        density,
+        lame,
+        shear,
+        jac,
+        nrm,
+        fscale,
+        deriv,
+        fproj,
+        lift,
+        nbr,
+        send,
+        cluster,
+        sea_face,
+        sea_cell,
+    ) = refs[21:36]
+    (
+        base,
+        tab,
+        tab2,
+        otail,
+        acc,
+        amat,
+        lmat,
+        sidx,
+        nbr8,
+        coef,
+        msg,
+        msg_in,
+        tails,
+        hand,
+        hand_in,
+        flow,
+        level,
+        flow_side,
+        flow_side_in,
+        flow_corner,
+        flow_corner_in,
+        level_side,
+        level_side_in,
+        level_corner_in,
+        local_sem,
+        send_sem,
+        recv_sem,
+    ) = refs[36:]
     devices = n_dom * n_tile
     dom, tile = lax.axis_index("dom"), lax.axis_index("tile")
     me = dom * n_tile + tile
@@ -106,32 +124,49 @@
     greet = offsets + [n_tile - 1, -(n_tile - 1)]
 
     def device(offset):
-        target = lax.rem(me + (offset + devices), devices)
-        return (target // n_tile, lax.rem(target, n_tile))
+        target = me + offset % devices
+        return jnp.where(target >= devices, target - devices, target)
 
     barrier = pltpu.get_barrier_semaphore()
     for o in greet:
-        pl.semaphore_signal(barrier, inc=1, device_id=device(o), device_id_type=MESH)
-
-    x_copy = pltpu.make_async_copy(dof, x_ref, local_sem.at[0])
-    x_copy.start()
-    grid_copies = []
+        pl.semaphore_signal(barrier, inc=1, device_id=device(o), device_id_type=FLAT)
+
+    near = {}
+
+    def fetch(name, src, dst):
+        near[name] = pltpu.make_async_copy(src, dst, local_sem.at[len(near)])
+        near[name].start()
+
+    fetch("deriv", deriv_in, deriv)
+    fetch("fproj", fproj_in, fproj)
+    fetch("lift", lift_in, lift)
+    for i in range(E // CH):
+        cut = slice(i * CH, (i + 1) * CH)
+        fetch(f"dof{i}", dof_in.at[:, :, cut], x_ref.at[:, :, cut])
+        if i == 0:
+            fetch("density", density_in, density)
+            fetch("lame", lame_in, lame)
+            fetch("shear", shear_in, shear)
+            fetch("jac", jac_in, jac)
+    fetch("sea_face", sea_face_in, sea_face)
+    fetch("send", send_in, send)
+    fetch("nbr", nbr_in, nbr)
+    fetch("nrm", nrm_in, nrm)
+    fetch("fscale", fscale_in, fscale)
+    fetch("cluster", cluster_in, cluster)
+    fetch("sea_cell", sea_cell_in, sea_cell)
+    grid_rows = slice(ROW0, ROW0 + 64)
     for t in range(4):
         lanes = slice(t * LANES, (t + 1) * LANES)
-        rows = slice(ROW0, ROW0 + 64)
-        grid_copies += [
-            pltpu.make_async_copy(
-                momentum.at[:, :, lanes], flow.at[0:2, t, rows, :], local_sem.at[1 + t]
-            ),
-            pltpu.make_async_copy(depth.at[:, lanes], flow.at[2, t, rows, :], local_sem.at[5 + t]),
-            pltpu.make_async_copy(height.at[:, lanes], level.at[t, rows, :], local_sem.at[9 + t]),
-        ]
-    for c in grid_copies:
-        c.start()
+        fetch(f"momentum{t}", momentum.at[:, :, lanes], flow.at[0:2, t, grid_rows, :])
+        fetch(f"depth{t}", depth.at[:, lanes], flow.at[2, t, grid_rows, :])
+        fetch(f"height{t}", height.at[:, lanes], level.at[t, grid_rows, :])
 
     lane = lax.broadcasted_iota(jnp.int32, (8, LANES), 1)
     sub = lax.broadcasted_iota(jnp.int32, (8, LANES), 0)
 
+    for name in ("deriv", "fproj", "lift"):
+        near[name].wait()
     amat[...] = jnp.zeros_like(amat)
     lmat[...] = jnp.zeros_like(lmat)
     for d in range(3):
@@ -158,25 +193,8 @@
     l_all = l_high + pltpu.roll(l_high, 40, 1) + pltpu.roll(l_low, 80, 1)
     l_all = l_all.astype(BF16)[:, 0:120]
 
-    inv_den = 1.0 / density[...]
-    speed = jnp.sqrt((lame[...] + 2.0 * shear[...]) * inv_den)
-    half = 0.5 * fscale[...]
-    scaled = [half * nrm[j] for j in range(3)]
-    coefs = (
-        scaled
-        + [shear[...] * s for s in scaled]
-        + [inv_den * s for s in scaled]
-        + [half * speed]
-    )
-    for k, c in enumerate(coefs):
-        for f in range(4):
-            coef[k, 2 * f : 2 * f + 2, :] = jnp.broadcast_to(c[f : f + 1, :], (2, E))
-    for f in range(4):
-        nbr8[2 * f : 2 * f + 2, :] = jnp.broadcast_to(nbr[f : f + 1, :], (2, E))
-    sidx[...] = jnp.zeros_like(sidx)
-    sidx[0:11, 0:SLOTS] = send[...]
-
-    x_copy.wait()
+    for name in ("density", "lame", "shear", "jac"):
+        near[name].wait()
 
     def predictor(i, _):
         off = pl.multiple_of(i * CH, CH)
@@ -238,7 +256,10 @@
                 tab2[j, :, here] = packed
         return 0
 
-    lax.fori_loop(0, E // CH, predictor, 0)
+    for i in range(E // CH):
+        near[f"dof{i}"].wait()
+        lax.fori_loop(i, i + 1, predictor, 0)
+    near["sea_face"].wait()
 
     shift = lax.rem(devices - me, devices)
     ups = [jnp.broadcast_to(tab[8, 0:1, t * LANES : (t + 1) * LANES], (8, LANES)) for t in range(4)]
@@ -266,7 +287,7 @@
             send_sem=send_sem.at[k],
             recv_sem=recv_sem.at[k],
             device_id=device(offset),
-            device_id_type=MESH,
+            device_id_type=FLAT,
         )
         copy.start()
         copies.append(copy)
@@ -278,6 +299,9 @@
         row = o // 8 * 8
         hand_copies.append(push(hand.at[row : row + 8, :], hand_in.at[k], o))
 
+    near["send"].wait()
+    sidx[...] = jnp.zeros_like(sidx)
+    sidx[0:11, 0:SLOTS] = send[...]
     def gather(sources, idx, tiles, start):
         at, which = idx & (LANES - 1), idx >> 7
         res = list(start)
@@ -312,31 +336,64 @@
         for n in members:
             dg_copies.append(push(msg.at[n], msg_in.at[n], offsets[n]))
 
-    for c in grid_copies:
-        c.wait()
-
-    def halos(ring, left, right):
-        lead = (slice(None),) * (len(ring.shape) - 3)
-        top, low = slice(ROW0, ROW0 + 8), slice(ROW0 + 56, ROW0 + 64)
-        above, below = slice(ROW0 - 8, ROW0), slice(ROW0 + 64, ROW0 + 72)
-        body = slice(ROW0, ROW0 + 64)
-        cols = slice(0, 4)
-        res = []
-        for offset, src, dst in (
-            (-n_tile, ring.at[lead + (cols, top)], ring.at[lead + (cols, below)]),
-            (n_tile, ring.at[lead + (cols, low)], ring.at[lead + (cols, above)]),
-            (-1, ring.at[lead + (0, body)], right.at[lead + (body,)]),
-            (1, ring.at[lead + (3, body)], left.at[lead + (body,)]),
-            (-n_tile - 1, ring.at[lead + (0, top)], right.at[lead + (below,)]),
-            (-n_tile + 1, ring.at[lead + (3, top)], left.at[lead + (below,)]),
-            (n_tile - 1, ring.at[lead + (0, low)], right.at[lead + (above,)]),
-            (n_tile + 1, ring.at[lead + (3, low)], left.at[lead + (above,)]),
-        ):
-            res.append(push(src, dst, offset))
+    for t in range(4):
+        near[f"momentum{t}"].wait()
+        near[f"depth{t}"].wait()
+        near[f"height{t}"].wait()
+    top, low = slice(ROW0, ROW0 + 8), slice(ROW0 + 56, ROW0 + 64)
+    above, below = slice(ROW0 - 8, ROW0), slice(ROW0 + 64, ROW0 + 72)
+    group = lane // 8
+
+    def column(ring, t):
+        res = None
+        for r in range(8):
+            val = ring[t, ROW0 + 8 * r : ROW0 + 8 * r + 8, :]
+            turn = (8 * r + (8 if t else 0)) % LANES
+            val = pltpu.roll(val, turn, 1) if turn else val
+            res = val if res is None else jnp.where(group == r, val, res)
         return res
 
-    flow_copies = halos(flow, flow_l, flow_r)
-
+    corners = ((0, top), (3, top), (0, low), (3, low))
+    for side, t in ((0, 0), (1, 3)):
+        fx, fy, dp = (column(flow.at[k], t) for k in range(3))
+        flow_side[side, 0] = jnp.where(lane < 64, fx, pltpu.roll(fy, 64, 1))
+        flow_side[side, 1] = dp
+    for k, (t, rows) in enumerate(corners):
+        turns = (0, 8, 16) if t == 0 else (0, LANES - 8, LANES - 16)
+        fx, fy, dp = (
+            pltpu.roll(flow[i, t, rows, :], turns[i], 1) if i else flow[i, t, rows, :]
+            for i in range(3)
+        )
+        spot = group if t == 0 else 15 - group
+        flow_corner[k] = jnp.where(spot == 0, fx, jnp.where(spot == 1, fy, dp))
+    corner_offsets = (-n_tile - 1, -n_tile + 1, n_tile - 1, n_tile + 1)
+    cols = slice(0, 4)
+    flow_copies = [
+        push(flow.at[:, cols, top, :], flow.at[:, cols, below, :], -n_tile),
+        push(flow.at[:, cols, low, :], flow.at[:, cols, above, :], n_tile),
+        push(flow_side.at[0], flow_side_in.at[0], -1),
+        push(flow_side.at[1], flow_side_in.at[1], 1),
+    ]
+    for k, o in enumerate(corner_offsets):
+        flow_copies.append(push(flow_corner.at[k], flow_corner_in.at[k], o))
+
+    for name in ("nbr", "nrm", "fscale", "cluster", "sea_cell"):
+        near[name].wait()
+    inv_den = 1.0 / density[...]
+    speed = jnp.sqrt((lame[...] + 2.0 * shear[...]) * inv_den)
+    half = 0.5 * fscale[...]
+    scaled = [half * nrm[j] for j in range(3)]
+    coefs = (
+        scaled
+        + [shear[...] * s for s in scaled]
+        + [inv_den * s for s in scaled]
+        + [half * speed]
+    )
+    for k, c in enumerate(coefs):
+        for f in range(4):
+            coef[k, 2 * f : 2 * f + 2, :] = jnp.broadcast_to(c[f : f + 1, :], (2, E))
+    for f in range(4):
+        nbr8[2 * f : 2 * f + 2, :] = jnp.broadcast_to(nbr[f : f + 1, :], (2, E))
     def local_gather(et, _):
         off = pl.multiple_of(et * LANES, LANES)
         for f in range(4):
@@ -379,88 +436,24 @@
     col_ids = lax.broadcasted_iota(jnp.int32, (64, E), 1)
     picks = []
     for k in range(4):
-        column = jnp.broadcast_to(cells[:, back[k] : back[k] + 1] & (E - 1), (64, E))
-        picks.append(jnp.where(col_ids == column, 1.0, 0.0).astype(BF16))
+        chosen = jnp.broadcast_to(cells[:, back[k] : back[k] + 1] & (E - 1), (64, E))
+        picks.append(jnp.where(col_ids == chosen, 1.0, 0.0).astype(BF16))
     lifted = jnp.dot(left, jnp.concatenate(picks, axis=0), preferred_element_type=F32)
     for t in range(4):
         lanes = slice(t * LANES, (t + 1) * LANES)
         level[t, ROW0 : ROW0 + 64, :] += lifted[0:64, lanes] + lifted[64:128, lanes]
-    level_copies = halos(level, level_l, level_r)
+    for side, t in ((0, 0), (1, 3)):
+        level_side[side] = column(level, t)
+    level_copies = [
+        push(level.at[cols, top, :], level.at[cols, below, :], -n_tile),
+        push(level.at[cols, low, :], level.at[cols, above, :], n_tile),
+        push(level_side.at[0], level_side_in.at[0], -1),
+        push(level_side.at[1], level_side_in.at[1], 1),
+    ]
+    for k, (o, (t, rows)) in enumerate(zip(corner_offsets, corners)):
+        level_copies.append(push(level.at[t, rows, :], level_corner_in.at[k], o))
 
     lax.fori_loop(2, 4, local_gather, 0)
-
-    for c in flow_copies:
-        c.wait()
-    above_ok = jnp.where(dom > 0, 1.0, 0.0)
-    below_ok = jnp.where(dom < n_dom - 1, 1.0, 0.0)
-    right_ok = jnp.where(tile < n_tile - 1, 1.0, 0.0)
-    left_ok = jnp.where(tile > 0, 1.0, 0.0)
-    span = slice(ROW0 - 8, ROW0 + 72)
-    lane80 = lax.broadcasted_iota(jnp.int32, (80, LANES), 1)
-    row80 = lax.broadcasted_iota(jnp.int32, (80, LANES), 0)
-    row_ok = jnp.where(row80 < 8, above_ok, jnp.where(row80 >= 72, below_ok, 1.0))
-    side_ok = row_ok * jnp.where(lane80 < 64, right_ok, left_ok)
-
-    def close(ring, left, right, scale):
-        for t in range(4):
-            ring[t, ROW0 - 8 : ROW0, :] = ring[t, ROW0 - 8 : ROW0, :] * above_ok
-            ring[t, ROW0 + 64 : ROW0 + 72, :] = ring[t, ROW0 + 64 : ROW0 + 72, :] * below_ok
-        ring[4, span, :] = jnp.where(lane80 < 64, right[span, :], left[span, :]) * side_ok
-        if scale is not None:
-            for t in range(5):
-                ring[t, span, :] = ring[t, span, :] * scale
-
-    c0 = 0.5 * WAVE_RATE
-    for k in range(3):
-        close(flow.at[k], flow_l.at[k], flow_r.at[k], c0 if k == 2 else None)
-    for c in level_copies:
-        c.wait()
-    close(level, level_l, level_r, None)
-    for ring in (flow.at[0], level):
-        for t in range(5):
-            ring[t, 0:8, :] = jnp.zeros((8, LANES), F32)
-            ring[t, ROWS - 8 : ROWS, :] = jnp.zeros((8, LANES), F32)
-    up, down = slice(ROW0 - 9, ROW0 + 71), slice(ROW0 - 7, ROW0 + 73)
-
-    def across(ring):
-        vals = [ring[t, span, :] for t in range(5)]
-        fwd = [pltpu.roll(x, LANES - 1, 1) for x in vals]
-        bwd = [pltpu.roll(x, 1, 1) for x in vals]
-        res = []
-        for t in range(5):
-            nxt = jnp.where(lane80 == LANES - 1, fwd[(t + 1) % 5], fwd[t])
-            prv = jnp.where(lane80 == 0, bwd[(t + 4) % 5], bwd[t])
-            res.append(nxt - prv)
-        return res
-
-    def wave(_, carry):
-        diff = across(flow.at[1])
-        for t in range(5):
-            spread = (flow[0, t, down, :] - flow[0, t, up, :]) + diff[t]
-            ok = side_ok if t == 4 else row_ok
-            level[t, span, :] = level[t, span, :] - (c0 * ok) * spread
-        diff = across(level)
-        for t in range(5):
-            g = flow[2, t, span, :]
-            flow[0, t, span, :] = flow[0, t, span, :] - g * (level[t, down, :] - level[t, up, :])
-            flow[1, t, span, :] = flow[1, t, span, :] - g * diff[t]
-        return carry
-
-    lax.fori_loop(0, STEPS, wave, 0)
-    out_copies = []
-    for t in range(4):
-        lanes = slice(t * LANES, (t + 1) * LANES)
-        rows = slice(ROW0, ROW0 + 64)
-        out_copies += [
-            pltpu.make_async_copy(
-                flow.at[0:2, t, rows, :], momentum_out.at[:, :, lanes], local_sem.at[1 + t]
-            ),
-            pltpu.make_async_copy(
-                level.at[t, rows, :], height_out.at[:, lanes], local_sem.at[9 + t]
-            ),
-        ]
-    for c in out_copies:
-        c.start()
 
     for c in dg_copies:
         c.wait_recv()
@@ -532,13 +525,127 @@
         return 0
 
     lax.fori_loop(0, E // LANES, finish, 0)
-    done = pltpu.make_async_copy(out, dof_out, local_sem.at[0])
-    done.start()
     for c in hand_copies + dg_copies:
         c.wait_send()
-    for c in out_copies:
+    for c in flow_copies:
         c.wait()
-    done.wait()
+    above_ok, below_ok, right_ok, left_ok = inside(n_dom, n_tile)
+
+    def close(ring, side, corner, res, scale):
+        for t in range(4):
+            res[t, ROW0 - 8 : ROW0, :] = ring[t, ROW0 - 8 : ROW0, :] * (above_ok * scale)
+            res[t, ROW0 + 64 : ROW0 + 72, :] = ring[t, ROW0 + 64 : ROW0 + 72, :] * (below_ok * scale)
+            val = ring[t, grid_rows, :]
+            res[t, grid_rows, :] = val * scale if scale != 1.0 else val
+        side_ok = jnp.where(lane < 64, right_ok, left_ok) * scale
+        for r in range(8):
+            right, left = side(r)
+            res[4, ROW0 + 8 * r : ROW0 + 8 * r + 8, :] = jnp.where(lane < 64, right, left) * side_ok
+        res[4, below, :] = jnp.where(lane < 64, corner(0), corner(1)) * (side_ok * below_ok)
+        res[4, above, :] = jnp.where(lane < 64, corner(2), corner(3)) * (side_ok * above_ok)
+        for t in range(5):
+            res[t, 0:8, :] = jnp.zeros((8, LANES), F32)
+            res[t, ROWS - 8 : ROWS, :] = jnp.zeros((8, LANES), F32)
+
+    def turned(val, turn):
+        return pltpu.roll(val, turn % LANES, 1) if turn % LANES else val
+
+    for k in range(3):
+        start = 64 if k == 1 else 0
+        from_right, from_left = flow_side_in[0, k // 2], flow_side_in[1, k // 2]
+
+        def side(r):
+            at = start + 8 * r
+            return turned(from_right, -at), turned(from_left, LANES - 8 - at)
+
+        def corner(j):
+            return turned(flow_corner_in[j], (-8 if j % 2 == 0 else 8) * k)
+
+        close(flow.at[k], side, corner, flow_out.at[k], 0.5 * WAVE_RATE if k == 2 else 1.0)
+    for c in level_copies:
+        c.wait()
+    from_right, from_left = level_side_in[0], level_side_in[1]
+
+    def level_sides(r):
+        return turned(from_right, -8 * r), turned(from_left, LANES - 8 - 8 * r)
+
+    close(level, level_sides, lambda j: level_corner_in[j], level_out, 1.0)
+
+
+def inside(n_dom, n_tile):
+    dom, tile = lax.axis_index("dom"), lax.axis_index("tile")
+    return (
+        jnp.where(dom > 0, 1.0, 0.0),
+        jnp.where(dom < n_dom - 1, 1.0, 0.0),
+        jnp.where(tile < n_tile - 1, 1.0, 0.0),
+        jnp.where(tile > 0, 1.0, 0.0),
+    )
+
+
+def grid_kernel(n_dom, n_tile, dof, flow_in, level_in, dof_out, height_out, momentum_out, *rest):
+    flow, level, sem = rest
+    dof_copy = pltpu.make_async_copy(dof, dof_out, sem.at[0])
+    dof_copy.start()
+    above_ok, below_ok, right_ok, left_ok = inside(n_dom, n_tile)
+    c0 = 0.5 * WAVE_RATE
+    lane = lax.broadcasted_iota(jnp.int32, (8, LANES), 1)
+    side_ok = jnp.where(lane < 64, right_ok, left_ok)
+    for ring in (flow.at[0], level):
+        for t in range(5):
+            ring[t, 0:8, :] = jnp.zeros((8, LANES), F32)
+            ring[t, ROWS - 8 : ROWS, :] = jnp.zeros((8, LANES), F32)
+
+    def across(vals):
+        fwd = [pltpu.roll(x, LANES - 1, 1) for x in vals]
+        bwd = [pltpu.roll(x, 1, 1) for x in vals]
+        res = []
+        for t in range(5):
+            nxt = jnp.where(lane == LANES - 1, fwd[(t + 1) % 5], fwd[t])
+            prv = jnp.where(lane == 0, bwd[(t + 4) % 5], bwd[t])
+            res.append(nxt - prv)
+        return res
+
+    def wave(flow_old, level_old):
+        for r in range(10):
+            at = ROW0 - 8 + 8 * r
+            rows = slice(at, at + 8)
+            row_ok = above_ok if r == 0 else below_ok if r == 9 else 1.0
+            diff = across([flow_old[1, t, rows, :] for t in range(5)])
+            for t in range(5):
+                spread = flow_old[0, t, at + 1 : at + 9, :] - flow_old[0, t, at - 1 : at + 7, :]
+                rate = c0 * row_ok * side_ok if t == 4 else c0 * row_ok
+                level[t, rows, :] = level_old[t, rows, :] - rate * (spread + diff[t])
+        for r in range(10):
+            at = ROW0 - 8 + 8 * r
+            rows = slice(at, at + 8)
+            diff = across([level[t, rows, :] for t in range(5)])
+            for t in range(5):
+                g = flow_in[2, t, rows, :]
+                slope = level[t, at + 1 : at + 9, :] - level[t, at - 1 : at + 7, :]
+                flow[0, t, rows, :] = flow_old[0, t, rows, :] - g * slope
+                flow[1, t, rows, :] = flow_old[1, t, rows, :] - g * diff[t]
+
+    wave(flow_in, level_in)
+
+    def again(_, carry):
+        wave(flow, level)
+        return carry
+
+    lax.fori_loop(0, STEPS - 1, again, 0)
+    copies = [dof_copy]
+    rows = slice(ROW0, ROW0 + 64)
+    for t in range(4):
+        lanes = slice(t * LANES, (t + 1) * LANES)
+        copies += [
+            pltpu.make_async_copy(
+                flow.at[:, t, rows, :], momentum_out.at[:, :, lanes], sem.at[1 + t]
+            ),
+            pltpu.make_async_copy(level.at[t, rows, :], height_out.at[:, lanes], sem.at[5 + t]),
+        ]
+    for c in copies[1:]:
+        c.start()
+    for c in copies:
+        c.wait()
 
 
 def shards(
@@ -564,47 +671,9 @@
     n_dom, n_tile = lax.axis_size("dom"), lax.axis_size("tile")
     row = lambda x: x.reshape(1, x.shape[0])
     vmem = pl.BlockSpec(memory_space=pltpu.VMEM)
-    far = pl.BlockSpec(memory_space=pl.ANY)
+    far = pl.BlockSpec(memory_space=pltpu.HBM)
     table = (TILES + RTILES) * LANES
-    dof_out, height_out, momentum_out = pl.pallas_call(
-        functools.partial(kernel, n_dom, n_tile),
-        out_shape=(
-            jax.ShapeDtypeStruct((Q, B, E), F32),
-            jax.ShapeDtypeStruct(height.shape, F32),
-            jax.ShapeDtypeStruct(momentum.shape, F32),
-        ),
-        in_specs=[far] + [vmem] * 14 + [far] * 3,
-        out_specs=(far, far, far),
-        scratch_shapes=[
-            pltpu.VMEM((Q, B, E), F32),
-            pltpu.VMEM((Q, BP, E), F32),
-            pltpu.VMEM((Q, B, E), F32),
-            pltpu.VMEM((2 * Q, 8, table), F32),
-            pltpu.VMEM((3, 8, TILES * LANES), F32),
-            pltpu.VMEM((Q, 8, E), F32),
-            pltpu.VMEM((Q, 8, 5 * E), F32),
-            pltpu.VMEM((144, LANES), F32),
-            pltpu.VMEM((LANES, LANES), F32),
-            pltpu.VMEM((16, LANES), jnp.int32),
-            pltpu.VMEM((8, E), jnp.int32),
-            pltpu.VMEM((10, 8, E), F32),
-            pltpu.VMEM((11, 24, LANES), F32),
-            pltpu.VMEM((11, 24, LANES), F32),
-            pltpu.VMEM((9, 8, LANES), F32),
-            pltpu.VMEM((LANES, LANES), F32),
-            pltpu.VMEM((3, 8, LANES), F32),
-            pltpu.VMEM((3, 5, ROWS, LANES), F32),
-            pltpu.VMEM((3, ROWS, LANES), F32),
-            pltpu.VMEM((3, ROWS, LANES), F32),
-            pltpu.VMEM((5, ROWS, LANES), F32),
-            pltpu.VMEM((ROWS, LANES), F32),
-            pltpu.VMEM((ROWS, LANES), F32),
-            pltpu.SemaphoreType.DMA((13,)),
-            pltpu.SemaphoreType.DMA((30,)),
-            pltpu.SemaphoreType.DMA((30,)),
-        ],
-        compiler_params=pltpu.CompilerParams(collective_id=0, has_side_effects=True),
-    )(
+    args = (
         jnp.transpose(dof_values, (1, 0, 2)),
         row(density),
         row(lame_lambda),
@@ -624,6 +693,65 @@
         momentum,
         ocean_depth,
     )
+    dof_new, flow, level = pl.pallas_call(
+        functools.partial(kernel, n_dom, n_tile),
+        out_shape=(
+            pltpu.VMEM((Q, B, E), F32),
+            pltpu.VMEM((3, 5, ROWS, LANES), F32),
+            pltpu.VMEM((5, ROWS, LANES), F32),
+        ),
+        in_specs=[far] * 18,
+        out_specs=(vmem,) * 3,
+        scratch_shapes=[pltpu.VMEM(x.shape, x.dtype) for x in args[:15]]
+        + [
+            pltpu.VMEM((Q, BP, E), F32),
+            pltpu.VMEM((2 * Q, 8, table), F32),
+            pltpu.VMEM((3, 8, TILES * LANES), F32),
+            pltpu.VMEM((Q, 8, E), F32),
+            pltpu.VMEM((Q, 8, 5 * E), F32),
+            pltpu.VMEM((144, LANES), F32),
+            pltpu.VMEM((LANES, LANES), F32),
+            pltpu.VMEM((16, LANES), jnp.int32),
+            pltpu.VMEM((8, E), jnp.int32),
+            pltpu.VMEM((10, 8, E), F32),
+            pltpu.VMEM((11, 24, LANES), F32),
+            pltpu.VMEM((11, 24, LANES), F32),
+            pltpu.VMEM((9, 8, LANES), F32),
+            pltpu.VMEM((LANES, LANES), F32),
+            pltpu.VMEM((3, 8, LANES), F32),
+            pltpu.VMEM((3, 5, ROWS, LANES), F32),
+            pltpu.VMEM((5, ROWS, LANES), F32),
+            pltpu.VMEM((2, 2, 8, LANES), F32),
+            pltpu.VMEM((2, 2, 8, LANES), F32),
+            pltpu.VMEM((4, 8, LANES), F32),
+            pltpu.VMEM((4, 8, LANES), F32),
+            pltpu.VMEM((2, 8, LANES), F32),
+            pltpu.VMEM((2, 8, LANES), F32),
+            pltpu.VMEM((4, 8, LANES), F32),
+            pltpu.SemaphoreType.DMA((32,)),
+            pltpu.SemaphoreType.DMA((30,)),
+            pltpu.SemaphoreType.DMA((30,)),
+        ],
+        compiler_params=pltpu.CompilerParams(
+            collective_id=0, has_side_effects=True, vmem_limit_bytes=VMEM
+        ),
+    )(*args)
+    dof_out, height_out, momentum_out = pl.pallas_call(
+        functools.partial(grid_kernel, n_dom, n_tile),
+        out_shape=(
+            jax.ShapeDtypeStruct((Q, B, E), F32),
+            jax.ShapeDtypeStruct(height.shape, F32),
+            jax.ShapeDtypeStruct(momentum.shape, F32),
+        ),
+        in_specs=[vmem] * 3,
+        out_specs=(far,) * 3,
+        scratch_shapes=[
+            pltpu.VMEM((2, 5, ROWS, LANES), F32),
+            pltpu.VMEM((5, ROWS, LANES), F32),
+            pltpu.SemaphoreType.DMA((9,)),
+        ],
+        compiler_params=pltpu.CompilerParams(vmem_limit_bytes=16 << 20),
+    )(dof_new, flow, level)
     return jnp.transpose(dof_out, (1, 0, 2)), height_out, momentum_out
 
 

time: 28.7 us -> 21.7 us (0.76)
  local copies, waits for them, and re-layouts: 3.54 us -> 0 us
  Pallas kernels: 24.2 us -> 20.7 us
    pallas_call x1 -> x2, Pallas kernels: 24.2 us -> 20.7 us  [the longest x1 18.6 us: shards(): pl.pallas_call(functools.partial(kernel, n_dom, n_tile), out_shape=(pltpu...]
    unnamed x7 -> x0, local copies, waits for them, and re-layouts: 3.54 us -> none
where the time goes in v2:
time: 21.7 us; the launch traced here: 21.3 us
  Pallas kernels  20.7 us (95%)
  between operations  0.65 us (3%)
    pallas_call x1, Pallas kernels, shards(): pl.pallas_call(functools.partial(kernel, n_dom, n_tile), out_shape=(pltpu...  18.6 us
    pallas_call x1, Pallas kernels, shards(): pl.pallas_call(functools.partial(grid_kernel, n_dom, n_tile), out_shape=(...  2.01 us

profile of v2, /device:TPU:1, one launch (start us, length us, event | category | flops | bytes accessed | tf_op | source)
XLA Modules:
  0.0 21.3 jit_solution(8942260298385186684)
XLA Ops:
  0.6 18.6 %shard_map.193 = (f32[9,20,512]{2,1,0:T(8,128)S(1)}, f32[3,5,96,128]{3,2,1,0:T(8,128)S(1)}, f32[5,96,128]{2,1,0:T(8,128)S(1)}) custom-call(f32[9,20,512]{2,1,0:T(8,128)} %bitcast.11, f32[1,512]{1,0:T(1,128)} %bitcast.17, f32[1,512]{1,0:T(1,128)} %bitcast.18, f32[1,512]{1,0:T(1,128)} %bitcast.19, f32[3,3,512]{2,1,0:T(4,128)} %refs_4_.1, ...), custom_call_target="tpu_custom_call" | custom-call | tf_op jit(solution)/shard_map/pallas_call | solution.py:696
  19.3 2.0 %shard_map.194 = (f32[9,20,512]{2,1,0:T(8,128)}, f32[64,512]{1,0:T(8,128)}, f32[2,64,512]{2,1,0:T(8,128)}) custom-call(f32[9,20,512]{2,1,0:T(8,128)S(1)} %get-tuple-element.9.dof, f32[3,5,96,128]{3,2,1,0:T(8,128)S(1)} %get-tuple-element.10.flow_in, f32[5,96,128]{2,1,0:T(8,128)S(1)} %get-tuple-element.11.level_in), custom_call_target="tpu_custom_call" | custom-call | tf_op jit(solution)/shard_map/pallas_call | solution.py:739

commit v3 on v2

--- a/solution.py
+++ b/solution.py
@@ -21,8 +21,12 @@
 Q = 9
 E = 512
 CH = 256
+GROUP = 2
+DOFS = 1
 LANES = 128
 VMEM = 58 << 20
+AHEAD = 1
+SIDE = 2
 TILES = 16
 RTILES = 3
 SLOTS = 32
@@ -140,8 +144,8 @@
     fetch("deriv", deriv_in, deriv)
     fetch("fproj", fproj_in, fproj)
     fetch("lift", lift_in, lift)
-    for i in range(E // CH):
-        cut = slice(i * CH, (i + 1) * CH)
+    for i in range(DOFS):
+        cut = slice(i * E // DOFS, (i + 1) * E // DOFS)
         fetch(f"dof{i}", dof_in.at[:, :, cut], x_ref.at[:, :, cut])
         if i == 0:
             fetch("density", density_in, density)
@@ -176,14 +180,14 @@
             row = fproj[c, f : f + 1, :]
             lrow = lift[c, f : f + 1, :]
             if c < 8:
-                amat[72 + f * 8 + c : 73 + f * 8 + c, 0:B] = row
+                amat[72 + f * 16 + c : 73 + f * 16 + c, 0:B] = row
                 lmat[f * 8 + c : f * 8 + c + 1, 0:B] = lrow
             else:
                 k = 32 + f * 2 + c - 8
-                amat[72 + k : 73 + k, 0:B] = row
+                amat[104 + k : 105 + k, 0:B] = row
                 lmat[k : k + 1, 0:B] = lrow
                 for r in range(4):
-                    k = 112 + f * 8 + r * 2 + c - 8
+                    k = 80 + f * 16 + r * 2 + c - 8
                     amat[k : k + 1, 0:B] = row
     a_high, a_low = split(amat[...])
     a_all = a_high + pltpu.roll(a_high, BP, 1) + pltpu.roll(a_low, 2 * BP, 1)
@@ -197,15 +201,35 @@
         near[name].wait()
 
     def predictor(i, _):
-        off = pl.multiple_of(i * CH, CH)
-        cut = pl.ds(off, CH)
-        rho = 1.0 / density[:, cut]
-        lam = lame[:, cut]
-        mu = shear[:, cut]
-        mu2 = mu + mu
-        jc = [[jac[d, x : x + 1, cut] for x in range(3)] for d in range(3)]
-
-        def combine(g):
+        chunks = []
+        for h in range(GROUP):
+            off = pl.multiple_of((i * GROUP + h) * CH, CH)
+            chunks.append(Chunk(off))
+        for k in range(1, 4):
+            for c in chunks:
+                c.advance(k)
+        for c in chunks:
+            c.finish()
+        return 0
+
+    class Chunk:
+        def __init__(self, off):
+            self.off = off
+            self.cut = cut = pl.ds(off, CH)
+            self.rho = 1.0 / density[:, cut]
+            self.lam = lame[:, cut]
+            self.mu = shear[:, cut]
+            self.jc = [[jac[d, x : x + 1, cut] for x in range(3)] for d in range(3)]
+            pad = jnp.zeros((BP - B, CH), F32)
+            self.term = [
+                STEP_SIZE * jnp.concatenate([x_ref[v, :, cut], pad], axis=0) for v in range(Q)
+            ]
+            self.integral = self.term
+
+        def combine(self, g, scale):
+            jc = [[x * scale for x in row] for row in self.jc] if scale != 1.0 else self.jc
+            lam, mu, rho = self.lam, self.mu, self.rho
+
             def phys(x, v):
                 return (
                     jc[0][x] * g[0:BP, v * CH : (v + 1) * CH]
@@ -215,50 +239,46 @@
 
             vg = [[phys(j, 6 + i) for j in range(3)] for i in range(3)]
             div = lam * (vg[0][0] + vg[1][1] + vg[2][2])
-            res = [div + mu2 * vg[i][i] for i in range(3)]
+            res = [div + (mu + mu) * vg[i][i] for i in range(3)]
             res += [mu * (vg[i][j] + vg[j][i]) for i, j in STRESS_ORDER[3:]]
             for i in range(3):
                 s = STRESS_PAIRS[i]
                 res.append(rho * (phys(0, s[0]) + phys(1, s[1]) + phys(2, s[2])))
             return res
 
-        pad = jnp.zeros((BP - B, CH), F32)
-        start = [jnp.concatenate([x_ref[v, :, cut], pad], axis=0) for v in range(Q)]
-        term = start
-        integral = [STEP_SIZE * w for w in term]
-        factor = STEP_SIZE
-        for k in range(1, 4):
-            right = stacked(jnp.concatenate(term, axis=1))
-            term = combine(jnp.dot(a_all[0:72], right, preferred_element_type=F32))
-            factor = factor * STEP_SIZE / (k + 1)
-            integral = [s + factor * w for s, w in zip(integral, term)]
-        right = stacked(jnp.concatenate(integral, axis=1))
-        g = jnp.dot(a_all, right, preferred_element_type=F32)
-        volume = combine(g)
-        for v in range(Q):
-            cols = slice(v * CH, (v + 1) * CH)
-            base[v, :, cut] = start[v] + volume[v]
+        def advance(self, k):
+            right = stacked(jnp.concatenate(self.term, axis=1))
+            g = jnp.dot(a_all[0:72], right, preferred_element_type=F32)
+            self.term = self.combine(g, STEP_SIZE / (k + 1))
+            self.integral = [s + w for s, w in zip(self.integral, self.term)]
+
+        def finish(self):
+            off, cut = self.off, self.cut
+            right = stacked(jnp.concatenate(self.integral, axis=1))
+            g = jnp.dot(a_all, right, preferred_element_type=F32)
+            volume = self.combine(g, 1.0)
+            for v in range(Q):
+                cols = slice(v * CH, (v + 1) * CH)
+                base[v, :, cut] = volume[v]
+                for f in range(4):
+                    here = pl.ds(pl.multiple_of(f * E + off, LANES), CH)
+                    tab[v, :, here] = g[72 + f * 16 : 80 + f * 16, cols]
+                    tab[Q + v, :, here] = g[80 + f * 16 : 88 + f * 16, cols]
+                otail[v, :, cut] = g[136:144, cols]
+            pair = lax.broadcasted_iota(jnp.int32, (8, CH), 0) // 2
             for f in range(4):
                 here = pl.ds(pl.multiple_of(f * E + off, LANES), CH)
-                tab[v, :, here] = g[72 + f * 8 : 80 + f * 8, cols]
-                tab[Q + v, :, here] = g[112 + f * 8 : 120 + f * 8, cols]
-            otail[v, :, cut] = g[104:112, cols]
-        for f in range(4):
-            here = pl.ds(pl.multiple_of(f * E + off, LANES), CH)
-            pair = lax.broadcasted_iota(jnp.int32, (8, CH), 0) // 2
-            for j in range(3):
-                packed = g[112 + f * 8 : 120 + f * 8, 4 * j * CH : (4 * j + 1) * CH]
-                for q in range(1, 4):
-                    if 4 * j + q < Q:
-                        v = 4 * j + q
-                        more = g[112 + f * 8 : 120 + f * 8, v * CH : (v + 1) * CH]
-                        packed = jnp.where(pair == q, more, packed)
-                tab2[j, :, here] = packed
-        return 0
-
-    for i in range(E // CH):
+                for j in range(3):
+                    packed = None
+                    for v in range(4 * j, min(4 * j + 4, Q)):
+                        val = g[80 + f * 16 : 88 + f * 16, v * CH : (v + 1) * CH]
+                        packed = val if packed is None else jnp.where(pair == v % 4, val, packed)
+                    tab2[j, :, here] = packed
+
+    per = E // (CH * GROUP)
+    for i in range(DOFS):
         near[f"dof{i}"].wait()
-        lax.fori_loop(i, i + 1, predictor, 0)
+        lax.fori_loop(i * per // DOFS, (i + 1) * per // DOFS, predictor, 0)
     near["sea_face"].wait()
 
     shift = lax.rem(devices - me, devices)
@@ -302,27 +322,32 @@
     near["send"].wait()
     sidx[...] = jnp.zeros_like(sidx)
     sidx[0:11, 0:SLOTS] = send[...]
-    def gather(sources, idx, tiles, start):
+    def gather(sources, idx, tiles):
         at, which = idx & (LANES - 1), idx >> 7
-        res = list(start)
+        res = [jnp.zeros((8, LANES), F32)] * len(sources)
         for t in tiles:
             mask = which == t
             for k, source in enumerate(sources):
                 val = jnp.take_along_axis(source[:, t * LANES : (t + 1) * LANES], at, axis=1)
-                res[k] = val if res[k] is None else jnp.where(mask, val, res[k])
+                res[k] = jnp.where(mask, val, res[k])
         return res
 
+    direct = range(TILES)
+    pair = sub // 2
     block = lane // SLOTS
     places = [(v // 4, v % 4) for v in range(Q)] + [(2, 1 + j) for j in range(3)]
     dg_copies = []
+    rows = []
     for p in range(RTILES):
-        members = [n for n in range(4 * p, 4 * p + 4) if n < len(offsets)]
         idx = jnp.zeros((8, LANES), jnp.int32)
-        for n in members:
+        for n in range(4 * p, min(4 * p + 4, len(offsets))):
             row = jnp.broadcast_to(sidx[n : n + 1, :], (8, LANES))
             idx = jnp.where(block == n % 4, pltpu.roll(row, SLOTS * (n % 4), 1), idx)
+        rows.append(idx)
+    for p in reversed(range(RTILES)):
+        members = [n for n in range(4 * p, 4 * p + 4) if n < len(offsets)]
         sources = [tab.at[v] for v in range(Q)] + [tab2.at[j] for j in range(3)]
-        got = gather(sources, idx, range(TILES), [None] * 12)
+        got = gather(sources, rows[p], direct)
         for n in members:
             for r in range(3):
                 packed = None
@@ -394,20 +419,23 @@
             coef[k, 2 * f : 2 * f + 2, :] = jnp.broadcast_to(c[f : f + 1, :], (2, E))
     for f in range(4):
         nbr8[2 * f : 2 * f + 2, :] = jnp.broadcast_to(nbr[f : f + 1, :], (2, E))
-    def local_gather(et, _):
-        off = pl.multiple_of(et * LANES, LANES)
-        for f in range(4):
-            idx = jnp.broadcast_to(nbr8[2 * f : 2 * f + 1, pl.ds(off, LANES)], (8, LANES))
-            got = gather([tab.at[v] for v in range(Q)], idx, range(TILES), [None] * Q)
-            for v in range(Q):
-                acc[v, :, pl.ds(pl.multiple_of(f * E + off, LANES), LANES)] = got[v]
-        idx = nbr8[:, pl.ds(off, LANES)]
-        got = gather([tab.at[Q + v] for v in range(Q)], idx, range(TILES), [None] * Q)
-        for v in range(Q):
-            acc[v, :, pl.ds(pl.multiple_of(4 * E + off, LANES), LANES)] = got[v]
+    def index(f, cut):
+        if f < 4:
+            return jnp.broadcast_to(nbr[f : f + 1, cut], (8, LANES))
+        return nbr8[:, cut]
+
+    def local_gather(i, _):
+        for et in range(AHEAD):
+            off = pl.multiple_of((i * AHEAD + et) * LANES, LANES)
+            cut = pl.ds(off, LANES)
+            for f in range(5):
+                here = pl.ds(pl.multiple_of(f * E + off, LANES), LANES)
+                got = gather([tab.at[v + Q * (f // 4)] for v in range(Q)], index(f, cut), direct)
+                for v in range(Q):
+                    acc[v, :, here] = got[v] - (tab[v, :, here] if f < 4 else otail[v, :, cut])
         return 0
 
-    lax.fori_loop(0, 2, local_gather, 0)
+    lax.fori_loop(0, 2 // AHEAD, local_gather, 0)
 
     for c in hand_copies:
         c.wait_recv()
@@ -453,13 +481,14 @@
     for k, (o, (t, rows)) in enumerate(zip(corner_offsets, corners)):
         level_copies.append(push(level.at[t, rows, :], level_corner_in.at[k], o))
 
-    lax.fori_loop(2, 4, local_gather, 0)
+    lax.fori_loop(2 // AHEAD, 4 // AHEAD, local_gather, 0)
 
     for c in dg_copies:
         c.wait_recv()
     for p in range(RTILES):
         members = [n for n in range(4 * p, 4 * p + 4) if n < len(offsets)]
         cols = slice((TILES + p) * LANES, (TILES + p + 1) * LANES)
+        unpacked = []
         for k, (pr, pb) in enumerate(places):
             res = None
             for n in members:
@@ -467,37 +496,28 @@
                 turn = (SLOTS * (n % 4 - pb)) % LANES
                 val = pltpu.roll(val, turn, 1) if turn else val
                 res = val if res is None else jnp.where(block == n % 4, val, res)
-            if k < Q:
-                tab[k, :, cols] = res
-            else:
-                tails[p * 3 + k - Q] = res
+            unpacked.append(res)
+        for j in range(3):
+            tails[p * 3 + j] = unpacked[Q + j]
         for v in range(Q):
             r = 2 * (v % 4)
             first = jnp.broadcast_to(tails[p * 3 + v // 4, r : r + 1, :], (8, LANES))
             second = jnp.broadcast_to(tails[p * 3 + v // 4, r + 1 : r + 2, :], (8, LANES))
+            tab[v, :, cols] = unpacked[v]
             tab[Q + v, :, cols] = jnp.where(sub % 2 == 0, first, second)
-
-    def finish(et, _):
-        off = pl.multiple_of(et * LANES, LANES)
+    def finish_one(off):
         cut = pl.ds(off, LANES)
         lam = lame[:, cut]
         remote = range(TILES, TILES + RTILES)
         parts = [[] for _ in range(Q)]
         for f in range(5):
             here = pl.ds(pl.multiple_of(f * E + off, LANES), LANES)
-            start = [acc[v, :, here] for v in range(Q)]
             if f < 4:
-                idx = jnp.broadcast_to(nbr8[2 * f : 2 * f + 1, cut], (8, LANES))
-                sources = [tab.at[v] for v in range(Q)]
-                own = [tab[v, :, here] for v in range(Q)]
                 c = [coef[k, 2 * f : 2 * f + 1, cut] for k in range(10)]
             else:
-                idx = nbr8[:, cut]
-                sources = [tab.at[Q + v] for v in range(Q)]
-                own = [otail[v, :, cut] for v in range(Q)]
                 c = [coef[k, :, cut] for k in range(10)]
-            got = gather(sources, idx, remote, start)
-            jump = [a - b for a, b in zip(got, own)]
+            got = gather([tab.at[v + Q * (f // 4)] for v in range(Q)], index(f, cut), remote)
+            jump = [acc[v, :, here] + got[v] for v in range(Q)]
             u = jump[6:9]
             n, mun, rhn, ws = c[0:3], c[3:6], c[6:9], c[9]
             flux = lam * (u[0] * n[0] + u[1] * n[1] + u[2] * n[2])
@@ -520,11 +540,16 @@
         lifts = jnp.dot(l_all, right, preferred_element_type=F32)
         chosen = jnp.broadcast_to(cluster[:, cut], (B, LANES)) == 1
         for v in range(Q):
-            new = base[v, 0:B, cut] + lifts[0:B, v * LANES : (v + 1) * LANES]
-            out[v, :, cut] = jnp.where(chosen, new, x_ref[v, :, cut])
+            x = x_ref[v, :, cut]
+            new = x + (base[v, 0:B, cut] + lifts[0:B, v * LANES : (v + 1) * LANES])
+            out[v, :, cut] = jnp.where(chosen, new, x)
+
+    def finish(i, _):
+        for et in range(SIDE):
+            finish_one(pl.multiple_of((i * SIDE + et) * LANES, LANES))
         return 0
 
-    lax.fori_loop(0, E // LANES, finish, 0)
+    lax.fori_loop(0, E // LANES // SIDE, finish, 0)
     for c in hand_copies + dg_copies:
         c.wait_send()
     for c in flow_copies:
@@ -605,7 +630,7 @@
             res.append(nxt - prv)
         return res
 
-    def wave(flow_old, level_old):
+    def rise(flow_old, level_old):
         for r in range(10):
             at = ROW0 - 8 + 8 * r
             rows = slice(at, at + 8)
@@ -615,15 +640,21 @@
                 spread = flow_old[0, t, at + 1 : at + 9, :] - flow_old[0, t, at - 1 : at + 7, :]
                 rate = c0 * row_ok * side_ok if t == 4 else c0 * row_ok
                 level[t, rows, :] = level_old[t, rows, :] - rate * (spread + diff[t])
+
+    def push(flow_old, t, at, diff):
+        rows = slice(at, at + 8)
+        g = flow_in[2, t, rows, :]
+        slope = level[t, at + 1 : at + 9, :] - level[t, at - 1 : at + 7, :]
+        flow[0, t, rows, :] = flow_old[0, t, rows, :] - g * slope
+        flow[1, t, rows, :] = flow_old[1, t, rows, :] - g * diff
+
+    def wave(flow_old, level_old):
+        rise(flow_old, level_old)
         for r in range(10):
             at = ROW0 - 8 + 8 * r
-            rows = slice(at, at + 8)
-            diff = across([level[t, rows, :] for t in range(5)])
+            diff = across([level[t, at : at + 8, :] for t in range(5)])
             for t in range(5):
-                g = flow_in[2, t, rows, :]
-                slope = level[t, at + 1 : at + 9, :] - level[t, at - 1 : at + 7, :]
-                flow[0, t, rows, :] = flow_old[0, t, rows, :] - g * slope
-                flow[1, t, rows, :] = flow_old[1, t, rows, :] - g * diff[t]
+                push(flow_old, t, at, diff[t])
 
     wave(flow_in, level_in)
 
@@ -631,19 +662,27 @@
         wave(flow, level)
         return carry
 
-    lax.fori_loop(0, STEPS - 1, again, 0)
+    lax.fori_loop(0, STEPS - 2, again, 0)
+    rise(flow, level)
     copies = [dof_copy]
     rows = slice(ROW0, ROW0 + 64)
+
+    def send(src, dst):
+        copies.append(pltpu.make_async_copy(src, dst, sem.at[len(copies)]))
+        copies[-1].start()
+
     for t in range(4):
-        lanes = slice(t * LANES, (t + 1) * LANES)
-        copies += [
-            pltpu.make_async_copy(
-                flow.at[:, t, rows, :], momentum_out.at[:, :, lanes], sem.at[1 + t]
-            ),
-            pltpu.make_async_copy(level.at[t, rows, :], height_out.at[:, lanes], sem.at[5 + t]),
-        ]
-    for c in copies[1:]:
-        c.start()
+        send(level.at[t, rows, :], height_out.at[:, t * LANES : (t + 1) * LANES])
+    for t in range(4):
+        for r in range(8):
+            at = ROW0 + 8 * r
+            here = level[t, at : at + 8, :]
+            ahead = level[t + 1, at : at + 8, :]
+            behind = level[(t + 4) % 5, at : at + 8, :]
+            nxt = jnp.where(lane == LANES - 1, pltpu.roll(ahead, LANES - 1, 1), pltpu.roll(here, LANES - 1, 1))
+            prv = jnp.where(lane == 0, pltpu.roll(behind, 1, 1), pltpu.roll(here, 1, 1))
+            push(flow, t, at, nxt - prv)
+        send(flow.at[:, t, rows, :], momentum_out.at[:, :, t * LANES : (t + 1) * LANES])
     for c in copies:
         c.wait()
 

time: 21.7 us -> 20.6 us (0.949); the launches traced: 21.3 us -> 20.5 us
  Pallas kernels: 20.7 us -> 19.9 us
    pallas_call x1, Pallas kernels: 18.6 us -> 17.7 us  [shards(): pl.pallas_call(functools.partial(kernel, n_dom, n_tile), out_shape=(pltpu...]
where the time goes in v3:
time: 20.6 us; the launch traced here: 20.5 us
  Pallas kernels  19.9 us (97%)
  between operations  0.65 us (3%)
    pallas_call x1, Pallas kernels, shards(): pl.pallas_call(functools.partial(kernel, n_dom, n_tile), out_shape=(pltpu...  17.7 us
    pallas_call x1, Pallas kernels, shards(): pl.pallas_call(functools.partial(grid_kernel, n_dom, n_tile), out_shape=(...  2.16 us

profile of v3, /device:TPU:1, one launch (start us, length us, event | category | flops | bytes accessed | tf_op | source)
XLA Modules:
  0.0 20.5 jit_solution(4798926027710107004)
XLA Ops:
  0.6 17.7 %shard_map.193 = (f32[9,20,512]{2,1,0:T(8,128)S(1)}, f32[3,5,96,128]{3,2,1,0:T(8,128)S(1)}, f32[5,96,128]{2,1,0:T(8,128)S(1)}) custom-call(f32[9,20,512]{2,1,0:T(8,128)} %bitcast.11, f32[1,512]{1,0:T(1,128)} %bitcast.17, f32[1,512]{1,0:T(1,128)} %bitcast.18, f32[1,512]{1,0:T(1,128)} %bitcast.19, f32[3,3,512]{2,1,0:T(4,128)} %refs_4_.1, ...), custom_call_target="tpu_custom_call" | custom-call | tf_op jit(solution)/shard_map/pallas_call | solution.py:735
  18.3 2.2 %shard_map.194 = (f32[9,20,512]{2,1,0:T(8,128)}, f32[64,512]{1,0:T(8,128)}, f32[2,64,512]{2,1,0:T(8,128)}) custom-call(f32[9,20,512]{2,1,0:T(8,128)S(1)} %get-tuple-element.9.dof, f32[3,5,96,128]{3,2,1,0:T(8,128)S(1)} %get-tuple-element.10.flow_in, f32[5,96,128]{2,1,0:T(8,128)S(1)} %get-tuple-element.11.level_in), custom_call_target="tpu_custom_call" | custom-call | tf_op jit(solution)/shard_map/pallas_call | solution.py:778

commit v4 on v3

--- a/solution.py
+++ b/solution.py
@@ -143,7 +143,6 @@
 
     fetch("deriv", deriv_in, deriv)
     fetch("fproj", fproj_in, fproj)
-    fetch("lift", lift_in, lift)
     for i in range(DOFS):
         cut = slice(i * E // DOFS, (i + 1) * E // DOFS)
         fetch(f"dof{i}", dof_in.at[:, :, cut], x_ref.at[:, :, cut])
@@ -158,45 +157,46 @@
     fetch("nrm", nrm_in, nrm)
     fetch("fscale", fscale_in, fscale)
     fetch("cluster", cluster_in, cluster)
+    fetch("lift", lift_in, lift)
     fetch("sea_cell", sea_cell_in, sea_cell)
     grid_rows = slice(ROW0, ROW0 + 64)
+    first = len(near)
     for t in range(4):
         lanes = slice(t * LANES, (t + 1) * LANES)
-        fetch(f"momentum{t}", momentum.at[:, :, lanes], flow.at[0:2, t, grid_rows, :])
-        fetch(f"depth{t}", depth.at[:, lanes], flow.at[2, t, grid_rows, :])
-        fetch(f"height{t}", height.at[:, lanes], level.at[t, grid_rows, :])
+        for k, (src, dst) in enumerate(
+            (
+                (momentum.at[:, :, lanes], flow.at[0:2, t, grid_rows, :]),
+                (depth.at[:, lanes], flow.at[2, t, grid_rows, :]),
+                (height.at[:, lanes], level.at[t, grid_rows, :]),
+            )
+        ):
+            pltpu.make_async_copy(src, dst, local_sem.at[first + k]).start()
+
+    def wait_all(ref, sem):
+        pltpu.make_async_copy(ref, ref, sem).wait()
 
     lane = lax.broadcasted_iota(jnp.int32, (8, LANES), 1)
     sub = lax.broadcasted_iota(jnp.int32, (8, LANES), 0)
 
-    for name in ("deriv", "fproj", "lift"):
+    for name in ("deriv", "fproj"):
         near[name].wait()
     amat[...] = jnp.zeros_like(amat)
-    lmat[...] = jnp.zeros_like(lmat)
     for d in range(3):
         amat[d * BP : d * BP + B, 0:B] = deriv[d]
     for f in range(4):
         for c in range(10):
             row = fproj[c, f : f + 1, :]
-            lrow = lift[c, f : f + 1, :]
             if c < 8:
                 amat[72 + f * 16 + c : 73 + f * 16 + c, 0:B] = row
-                lmat[f * 8 + c : f * 8 + c + 1, 0:B] = lrow
             else:
                 k = 32 + f * 2 + c - 8
                 amat[104 + k : 105 + k, 0:B] = row
-                lmat[k : k + 1, 0:B] = lrow
                 for r in range(4):
                     k = 80 + f * 16 + r * 2 + c - 8
                     amat[k : k + 1, 0:B] = row
     a_high, a_low = split(amat[...])
     a_all = a_high + pltpu.roll(a_high, BP, 1) + pltpu.roll(a_low, 2 * BP, 1)
     a_all = a_all.astype(BF16)[:, 0:80]
-    l_high, l_low = split(jnp.transpose(lmat[...]))
-    l_high, l_low = l_high[0:BP], l_low[0:BP]
-    l_all = l_high + pltpu.roll(l_high, 40, 1) + pltpu.roll(l_low, 80, 1)
-    l_all = l_all.astype(BF16)[:, 0:120]
-
     for name in ("density", "lame", "shear", "jac"):
         near[name].wait()
 
@@ -297,27 +297,20 @@
 
     pl.semaphore_wait(barrier, len(greet))
 
-    copies = []
-
-    def push(src, dst, offset):
-        k = len(copies)
-        copy = pltpu.make_async_remote_copy(
+    def push(src, dst, offset, group):
+        pltpu.make_async_remote_copy(
             src_ref=src,
             dst_ref=dst,
-            send_sem=send_sem.at[k],
-            recv_sem=recv_sem.at[k],
+            send_sem=send_sem.at[group],
+            recv_sem=recv_sem.at[group],
             device_id=device(offset),
             device_id_type=FLAT,
-        )
-        copy.start()
-        copies.append(copy)
-        return copy
+        ).start()
 
     hand_offsets = (1, n_tile, devices // 2)
-    hand_copies = []
     for k, o in enumerate(hand_offsets):
         row = o // 8 * 8
-        hand_copies.append(push(hand.at[row : row + 8, :], hand_in.at[k], o))
+        push(hand.at[row : row + 8, :], hand_in.at[k], o, 0)
 
     near["send"].wait()
     sidx[...] = jnp.zeros_like(sidx)
@@ -336,7 +329,6 @@
     pair = sub // 2
     block = lane // SLOTS
     places = [(v // 4, v % 4) for v in range(Q)] + [(2, 1 + j) for j in range(3)]
-    dg_copies = []
     rows = []
     for p in range(RTILES):
         idx = jnp.zeros((8, LANES), jnp.int32)
@@ -359,12 +351,11 @@
                     packed = val if packed is None else jnp.where(block == pb, val, packed)
                 msg[n, r * 8 : r * 8 + 8, :] = packed
         for n in members:
-            dg_copies.append(push(msg.at[n], msg_in.at[n], offsets[n]))
-
-    for t in range(4):
-        near[f"momentum{t}"].wait()
-        near[f"depth{t}"].wait()
-        near[f"height{t}"].wait()
+            push(msg.at[n], msg_in.at[n], offsets[n], 1)
+
+    wait_all(flow.at[0:2, 0:4, grid_rows, :], local_sem.at[first])
+    wait_all(flow.at[2, 0:4, grid_rows, :], local_sem.at[first + 1])
+    wait_all(level.at[0:4, grid_rows, :], local_sem.at[first + 2])
     top, low = slice(ROW0, ROW0 + 8), slice(ROW0 + 56, ROW0 + 64)
     above, below = slice(ROW0 - 8, ROW0), slice(ROW0 + 64, ROW0 + 72)
     group = lane // 8
@@ -393,17 +384,24 @@
         flow_corner[k] = jnp.where(spot == 0, fx, jnp.where(spot == 1, fy, dp))
     corner_offsets = (-n_tile - 1, -n_tile + 1, n_tile - 1, n_tile + 1)
     cols = slice(0, 4)
-    flow_copies = [
-        push(flow.at[:, cols, top, :], flow.at[:, cols, below, :], -n_tile),
-        push(flow.at[:, cols, low, :], flow.at[:, cols, above, :], n_tile),
-        push(flow_side.at[0], flow_side_in.at[0], -1),
-        push(flow_side.at[1], flow_side_in.at[1], 1),
-    ]
+    push(flow.at[:, cols, top, :], flow.at[:, cols, below, :], -n_tile, 2)
+    push(flow.at[:, cols, low, :], flow.at[:, cols, above, :], n_tile, 2)
+    push(flow_side.at[0], flow_side_in.at[0], -1, 2)
+    push(flow_side.at[1], flow_side_in.at[1], 1, 2)
     for k, o in enumerate(corner_offsets):
-        flow_copies.append(push(flow_corner.at[k], flow_corner_in.at[k], o))
-
-    for name in ("nbr", "nrm", "fscale", "cluster", "sea_cell"):
+        push(flow_corner.at[k], flow_corner_in.at[k], o, 2)
+
+    for name in ("nbr", "nrm", "fscale", "cluster", "sea_cell", "lift"):
         near[name].wait()
+    lmat[...] = jnp.zeros_like(lmat)
+    for f in range(4):
+        for c in range(10):
+            k = f * 8 + c if c < 8 else 32 + f * 2 + c - 8
+            lmat[k : k + 1, 0:B] = lift[c, f : f + 1, :]
+    l_high, l_low = split(jnp.transpose(lmat[...]))
+    l_high, l_low = l_high[0:BP], l_low[0:BP]
+    l_all = l_high + pltpu.roll(l_high, 40, 1) + pltpu.roll(l_low, 80, 1)
+    l_all = l_all.astype(BF16)[:, 0:120]
     inv_den = 1.0 / density[...]
     speed = jnp.sqrt((lame[...] + 2.0 * shear[...]) * inv_den)
     half = 0.5 * fscale[...]
@@ -437,8 +435,7 @@
 
     lax.fori_loop(0, 2 // AHEAD, local_gather, 0)
 
-    for c in hand_copies:
-        c.wait_recv()
+    wait_all(hand_in, recv_sem.at[0])
     back = (0, devices - 1, devices - n_tile, devices // 2)
     cells = pltpu.roll(sea_cell[...], shift, 1)
     cells_t = jnp.transpose(
@@ -472,19 +469,58 @@
         level[t, ROW0 : ROW0 + 64, :] += lifted[0:64, lanes] + lifted[64:128, lanes]
     for side, t in ((0, 0), (1, 3)):
         level_side[side] = column(level, t)
-    level_copies = [
-        push(level.at[cols, top, :], level.at[cols, below, :], -n_tile),
-        push(level.at[cols, low, :], level.at[cols, above, :], n_tile),
-        push(level_side.at[0], level_side_in.at[0], -1),
-        push(level_side.at[1], level_side_in.at[1], 1),
-    ]
+    push(level.at[cols, top, :], level.at[cols, below, :], -n_tile, 3)
+    push(level.at[cols, low, :], level.at[cols, above, :], n_tile, 3)
+    push(level_side.at[0], level_side_in.at[0], -1, 3)
+    push(level_side.at[1], level_side_in.at[1], 1, 3)
     for k, (o, (t, rows)) in enumerate(zip(corner_offsets, corners)):
-        level_copies.append(push(level.at[t, rows, :], level_corner_in.at[k], o))
+        push(level.at[t, rows, :], level_corner_in.at[k], o, 3)
 
     lax.fori_loop(2 // AHEAD, 4 // AHEAD, local_gather, 0)
 
-    for c in dg_copies:
-        c.wait_recv()
+    halo_bytes = flow.at[0, 0:4, 0:64, :]
+    wait_all(halo_bytes, recv_sem.at[2])
+    wait_all(halo_bytes, send_sem.at[2])
+    above_ok, below_ok, right_ok, left_ok = inside(n_dom, n_tile)
+
+    def close(ring, side, corner, res, scale):
+        for t in range(4):
+            res[t, ROW0 - 8 : ROW0, :] = ring[t, ROW0 - 8 : ROW0, :] * (above_ok * scale)
+            res[t, ROW0 + 64 : ROW0 + 72, :] = ring[t, ROW0 + 64 : ROW0 + 72, :] * (below_ok * scale)
+            val = ring[t, grid_rows, :]
+            res[t, grid_rows, :] = val * scale if scale != 1.0 else val
+        side_ok = jnp.where(lane < 64, right_ok, left_ok) * scale
+        for r in range(8):
+            right, left = side(r)
+            res[4, ROW0 + 8 * r : ROW0 + 8 * r + 8, :] = jnp.where(lane < 64, right, left) * side_ok
+        res[4, below, :] = jnp.where(lane < 64, corner(0), corner(1)) * (side_ok * below_ok)
+        res[4, above, :] = jnp.where(lane < 64, corner(2), corner(3)) * (side_ok * above_ok)
+        for t in range(5):
+            res[t, 0:8, :] = jnp.zeros((8, LANES), F32)
+            res[t, ROWS - 8 : ROWS, :] = jnp.zeros((8, LANES), F32)
+
+    def turned(val, turn):
+        return pltpu.roll(val, turn % LANES, 1) if turn % LANES else val
+
+    for k in range(3):
+        start = 64 if k == 1 else 0
+        from_right, from_left = flow_side_in[0, k // 2], flow_side_in[1, k // 2]
+
+        def side(r):
+            at = start + 8 * r
+            return turned(from_right, -at), turned(from_left, LANES - 8 - at)
+
+        def corner(j):
+            return turned(flow_corner_in[j], (-8 if j % 2 == 0 else 8) * k)
+
+        close(flow.at[k], side, corner, flow_out.at[k], 0.5 * WAVE_RATE if k == 2 else 1.0)
+    for k, to in ((1, 1), (2, 3)):
+        for r in range(10):
+            rows = slice(ROW0 - 8 + 8 * r, ROW0 + 8 * r)
+            spun = [pltpu.roll(flow_out[k, t, rows, :], 1, 1) for t in range(5)]
+            for t in range(5):
+                flow_out[to, t, rows, :] = jnp.where(lane == 0, spun[(t + 4) % 5], spun[t])
+    wait_all(msg_in, recv_sem.at[1])
     for p in range(RTILES):
         members = [n for n in range(4 * p, 4 * p + 4) if n < len(offsets)]
         cols = slice((TILES + p) * LANES, (TILES + p + 1) * LANES)
@@ -550,45 +586,11 @@
         return 0
 
     lax.fori_loop(0, E // LANES // SIDE, finish, 0)
-    for c in hand_copies + dg_copies:
-        c.wait_send()
-    for c in flow_copies:
-        c.wait()
-    above_ok, below_ok, right_ok, left_ok = inside(n_dom, n_tile)
-
-    def close(ring, side, corner, res, scale):
-        for t in range(4):
-            res[t, ROW0 - 8 : ROW0, :] = ring[t, ROW0 - 8 : ROW0, :] * (above_ok * scale)
-            res[t, ROW0 + 64 : ROW0 + 72, :] = ring[t, ROW0 + 64 : ROW0 + 72, :] * (below_ok * scale)
-            val = ring[t, grid_rows, :]
-            res[t, grid_rows, :] = val * scale if scale != 1.0 else val
-        side_ok = jnp.where(lane < 64, right_ok, left_ok) * scale
-        for r in range(8):
-            right, left = side(r)
-            res[4, ROW0 + 8 * r : ROW0 + 8 * r + 8, :] = jnp.where(lane < 64, right, left) * side_ok
-        res[4, below, :] = jnp.where(lane < 64, corner(0), corner(1)) * (side_ok * below_ok)
-        res[4, above, :] = jnp.where(lane < 64, corner(2), corner(3)) * (side_ok * above_ok)
-        for t in range(5):
-            res[t, 0:8, :] = jnp.zeros((8, LANES), F32)
-            res[t, ROWS - 8 : ROWS, :] = jnp.zeros((8, LANES), F32)
-
-    def turned(val, turn):
-        return pltpu.roll(val, turn % LANES, 1) if turn % LANES else val
-
-    for k in range(3):
-        start = 64 if k == 1 else 0
-        from_right, from_left = flow_side_in[0, k // 2], flow_side_in[1, k // 2]
-
-        def side(r):
-            at = start + 8 * r
-            return turned(from_right, -at), turned(from_left, LANES - 8 - at)
-
-        def corner(j):
-            return turned(flow_corner_in[j], (-8 if j % 2 == 0 else 8) * k)
-
-        close(flow.at[k], side, corner, flow_out.at[k], 0.5 * WAVE_RATE if k == 2 else 1.0)
-    for c in level_copies:
-        c.wait()
+    halo_bytes = level.at[0:2, 0:56, :]
+    wait_all(halo_bytes, recv_sem.at[3])
+    wait_all(halo_bytes, send_sem.at[3])
+    wait_all(hand_in, send_sem.at[0])
+    wait_all(msg, send_sem.at[1])
     from_right, from_left = level_side_in[0], level_side_in[1]
 
     def level_sides(r):
@@ -620,41 +622,44 @@
             ring[t, 0:8, :] = jnp.zeros((8, LANES), F32)
             ring[t, ROWS - 8 : ROWS, :] = jnp.zeros((8, LANES), F32)
 
-    def across(vals):
-        fwd = [pltpu.roll(x, LANES - 1, 1) for x in vals]
-        bwd = [pltpu.roll(x, 1, 1) for x in vals]
+    def turned(vals, turn):
+        spun = [pltpu.roll(x, -turn % LANES, 1) for x in vals]
+        edge = lane >= LANES - turn if turn > 0 else lane < -turn
+        step = 1 if turn > 0 else 4
+        return [jnp.where(edge, spun[(t + step) % 5], spun[t]) for t in range(5)]
+
+    def block(r):
+        at = ROW0 - 8 + 8 * r
+        return at, slice(at, at + 8)
+
+    def rise(r, flow_old, level_old):
+        at, rows = block(r)
+        row_ok = above_ok if r == 0 else below_ok if r == 9 else 1.0
+        vals = [flow_old[1, t, rows, :] for t in range(5)]
+        later = turned(vals, 2)
+        for t in range(5):
+            spread = flow_old[0, t, at + 1 : at + 9, :] - flow_old[0, t, at - 1 : at + 7, :]
+            rate = c0 * row_ok * side_ok if t == 4 else c0 * row_ok
+            level[t, rows, :] = level_old[t, rows, :] - rate * (spread + (later[t] - vals[t]))
+
+    def push(r, flow_old, last=False):
+        at, rows = block(r)
+        vals = [level[t, rows, :] for t in range(5)]
+        before = turned(vals, -2)
         res = []
         for t in range(5):
-            nxt = jnp.where(lane == LANES - 1, fwd[(t + 1) % 5], fwd[t])
-            prv = jnp.where(lane == 0, bwd[(t + 4) % 5], bwd[t])
-            res.append(nxt - prv)
-        return res
-
-    def rise(flow_old, level_old):
+            if t < 4 or not last:
+                slope = level[t, at + 1 : at + 9, :] - level[t, at - 1 : at + 7, :]
+                flow[0, t, rows, :] = flow_old[0, t, rows, :] - flow_in[2, t, rows, :] * slope
+            res.append(flow_old[1, t, rows, :] - flow_in[3, t, rows, :] * (vals[t] - before[t]))
+        for t, val in enumerate(turned(res, 1) if last else res):
+            flow[1, t, rows, :] = val
+
+    def wave(flow_old, level_old):
         for r in range(10):
-            at = ROW0 - 8 + 8 * r
-            rows = slice(at, at + 8)
-            row_ok = above_ok if r == 0 else below_ok if r == 9 else 1.0
-            diff = across([flow_old[1, t, rows, :] for t in range(5)])
-            for t in range(5):
-                spread = flow_old[0, t, at + 1 : at + 9, :] - flow_old[0, t, at - 1 : at + 7, :]
-                rate = c0 * row_ok * side_ok if t == 4 else c0 * row_ok
-                level[t, rows, :] = level_old[t, rows, :] - rate * (spread + diff[t])
-
-    def push(flow_old, t, at, diff):
-        rows = slice(at, at + 8)
-        g = flow_in[2, t, rows, :]
-        slope = level[t, at + 1 : at + 9, :] - level[t, at - 1 : at + 7, :]
-        flow[0, t, rows, :] = flow_old[0, t, rows, :] - g * slope
-        flow[1, t, rows, :] = flow_old[1, t, rows, :] - g * diff
-
-    def wave(flow_old, level_old):
-        rise(flow_old, level_old)
+            rise(r, flow_old, level_old)
         for r in range(10):
-            at = ROW0 - 8 + 8 * r
-            diff = across([level[t, at : at + 8, :] for t in range(5)])
-            for t in range(5):
-                push(flow_old, t, at, diff[t])
+            push(r, flow_old)
 
     wave(flow_in, level_in)
 
@@ -663,26 +668,25 @@
         return carry
 
     lax.fori_loop(0, STEPS - 2, again, 0)
-    rise(flow, level)
+    for r in range(10):
+        rise(r, flow, level)
     copies = [dof_copy]
-    rows = slice(ROW0, ROW0 + 64)
 
     def send(src, dst):
         copies.append(pltpu.make_async_copy(src, dst, sem.at[len(copies)]))
         copies[-1].start()
 
     for t in range(4):
-        send(level.at[t, rows, :], height_out.at[:, t * LANES : (t + 1) * LANES])
-    for t in range(4):
-        for r in range(8):
-            at = ROW0 + 8 * r
-            here = level[t, at : at + 8, :]
-            ahead = level[t + 1, at : at + 8, :]
-            behind = level[(t + 4) % 5, at : at + 8, :]
-            nxt = jnp.where(lane == LANES - 1, pltpu.roll(ahead, LANES - 1, 1), pltpu.roll(here, LANES - 1, 1))
-            prv = jnp.where(lane == 0, pltpu.roll(behind, 1, 1), pltpu.roll(here, 1, 1))
-            push(flow, t, at, nxt - prv)
-        send(flow.at[:, t, rows, :], momentum_out.at[:, :, t * LANES : (t + 1) * LANES])
+        lanes = slice(t * LANES, (t + 1) * LANES)
+        send(level.at[t, ROW0 : ROW0 + 64, :], height_out.at[:, lanes])
+    for part in range(2):
+        for r in range(4 * part, 4 * part + 4):
+            push(r + 1, flow, last=True)
+        rows = slice(32 * part, 32 * part + 32)
+        for t in range(4):
+            lanes = slice(t * LANES, (t + 1) * LANES)
+            ring = slice(ROW0 + 32 * part, ROW0 + 32 * part + 32)
+            send(flow.at[:, t, ring, :], momentum_out.at[:, rows, lanes])
     for c in copies:
         c.wait()
 
@@ -736,7 +740,7 @@
         functools.partial(kernel, n_dom, n_tile),
         out_shape=(
             pltpu.VMEM((Q, B, E), F32),
-            pltpu.VMEM((3, 5, ROWS, LANES), F32),
+            pltpu.VMEM((4, 5, ROWS, LANES), F32),
             pltpu.VMEM((5, ROWS, LANES), F32),
         ),
         in_specs=[far] * 18,
@@ -767,9 +771,9 @@
             pltpu.VMEM((2, 8, LANES), F32),
             pltpu.VMEM((2, 8, LANES), F32),
             pltpu.VMEM((4, 8, LANES), F32),
-            pltpu.SemaphoreType.DMA((32,)),
-            pltpu.SemaphoreType.DMA((30,)),
-            pltpu.SemaphoreType.DMA((30,)),
+            pltpu.SemaphoreType.DMA((18,)),
+            pltpu.SemaphoreType.DMA((4,)),
+            pltpu.SemaphoreType.DMA((4,)),
         ],
         compiler_params=pltpu.CompilerParams(
             collective_id=0, has_side_effects=True, vmem_limit_bytes=VMEM
@@ -787,7 +791,7 @@
         scratch_shapes=[
             pltpu.VMEM((2, 5, ROWS, LANES), F32),
             pltpu.VMEM((5, ROWS, LANES), F32),
-            pltpu.SemaphoreType.DMA((9,)),
+            pltpu.SemaphoreType.DMA((13,)),
         ],
         compiler_params=pltpu.CompilerParams(vmem_limit_bytes=16 << 20),
     )(dof_new, flow, level)

time: 20.6 us -> 19.9 us (0.966)
  Pallas kernels: 19.9 us -> 19.1 us
    pallas_call x1, Pallas kernels: 17.7 us -> 17.2 us  [shards(): pl.pallas_call(functools.partial(kernel, n_dom, n_tile), out_shape=(pltpu...]
    pallas_call x1, Pallas kernels: 2.16 us -> 1.87 us  [shards(): pl.pallas_call(functools.partial(grid_kernel, n_dom, n_tile), out_shape=(...]
where the time goes in v4:
time: 19.9 us; the launch traced here: 19.7 us
  Pallas kernels  19.1 us (96%)
  between operations  0.65 us (3%)
    pallas_call x1, Pallas kernels, shards(): pl.pallas_call(functools.partial(kernel, n_dom, n_tile), out_shape=(pltpu...  17.2 us
    pallas_call x1, Pallas kernels, shards(): pl.pallas_call(functools.partial(grid_kernel, n_dom, n_tile), out_shape=(...  1.87 us

profile of v4, /device:TPU:1, one launch (start us, length us, event | category | flops | bytes accessed | tf_op | source)
XLA Modules:
  0.0 19.7 jit_solution(7778375567385929224)
XLA Ops:
  0.6 17.2 %shard_map.193 = (f32[9,20,512]{2,1,0:T(8,128)S(1)}, f32[4,5,96,128]{3,2,1,0:T(8,128)S(1)}, f32[5,96,128]{2,1,0:T(8,128)S(1)}) custom-call(f32[9,20,512]{2,1,0:T(8,128)} %bitcast.11, f32[1,512]{1,0:T(1,128)} %bitcast.17, f32[1,512]{1,0:T(1,128)} %bitcast.18, f32[1,512]{1,0:T(1,128)} %bitcast.19, f32[3,3,512]{2,1,0:T(4,128)} %refs_4_.1, ...), custom_call_target="tpu_custom_call" | custom-call | tf_op jit(solution)/shard_map/pallas_call | solution.py:739
  17.9 1.9 %shard_map.194 = (f32[9,20,512]{2,1,0:T(8,128)}, f32[64,512]{1,0:T(8,128)}, f32[2,64,512]{2,1,0:T(8,128)}) custom-call(f32[9,20,512]{2,1,0:T(8,128)S(1)} %get-tuple-element.9.dof, f32[4,5,96,128]{3,2,1,0:T(8,128)S(1)} %get-tuple-element.10.flow_in, f32[5,96,128]{2,1,0:T(8,128)S(1)} %get-tuple-element.11.level_in), custom_call_target="tpu_custom_call" | custom-call | tf_op jit(solution)/shard_map/pallas_call | solution.py:782

commit v5 on v4

--- a/solution.py
+++ b/solution.py
@@ -25,8 +25,7 @@
 DOFS = 1
 LANES = 128
 VMEM = 58 << 20
-AHEAD = 1
-SIDE = 2
+SIDE = 4
 TILES = 16
 RTILES = 3
 SLOTS = 32
@@ -131,10 +130,6 @@
         target = me + offset % devices
         return jnp.where(target >= devices, target - devices, target)
 
-    barrier = pltpu.get_barrier_semaphore()
-    for o in greet:
-        pl.semaphore_signal(barrier, inc=1, device_id=device(o), device_id_type=FLAT)
-
     near = {}
 
     def fetch(name, src, dst):
@@ -151,6 +146,9 @@
             fetch("lame", lame_in, lame)
             fetch("shear", shear_in, shear)
             fetch("jac", jac_in, jac)
+    barrier = pltpu.get_barrier_semaphore()
+    for o in greet:
+        pl.semaphore_signal(barrier, inc=1, device_id=device(o), device_id_type=FLAT)
     fetch("sea_face", sea_face_in, sea_face)
     fetch("send", send_in, send)
     fetch("nbr", nbr_in, nbr)
@@ -295,6 +293,39 @@
     zeros64 = jnp.zeros((64, LANES), F32)
     hand[...] = jnp.transpose(jnp.concatenate([handed, zeros64], axis=0))
 
+    def gather(sources, idx, tiles):
+        at, which = idx & (LANES - 1), idx >> 7
+        res = [jnp.zeros((8, LANES), F32)] * len(sources)
+        for t in tiles:
+            mask = which == t
+            for k, source in enumerate(sources):
+                val = jnp.take_along_axis(source[:, t * LANES : (t + 1) * LANES], at, axis=1)
+                res[k] = jnp.where(mask, val, res[k])
+        return res
+
+    direct = range(TILES)
+    pair = sub // 2
+    def index(f, cut):
+        if f < 4:
+            return jnp.broadcast_to(nbr[f : f + 1, cut], (8, LANES))
+        return nbr8[:, cut]
+
+    def local_gather(et, _):
+        off = pl.multiple_of(et * LANES, LANES)
+        cut = pl.ds(off, LANES)
+        for f in range(5):
+            here = pl.ds(pl.multiple_of(f * E + off, LANES), LANES)
+            got = gather([tab.at[v + Q * (f // 4)] for v in range(Q)], index(f, cut), direct)
+            for v in range(Q):
+                acc[v, :, here] = got[v] - (tab[v, :, here] if f < 4 else otail[v, :, cut])
+        return 0
+
+    near["nbr"].wait()
+    for f in range(4):
+        nbr8[2 * f : 2 * f + 2, :] = jnp.broadcast_to(nbr[f : f + 1, :], (2, E))
+    ahead = jnp.where(dom == 0, 4, jnp.where(dom == 1, 3, 0))
+    lax.fori_loop(0, ahead, local_gather, 0)
+
     pl.semaphore_wait(barrier, len(greet))
 
     def push(src, dst, offset, group):
@@ -312,21 +343,47 @@
         row = o // 8 * 8
         push(hand.at[row : row + 8, :], hand_in.at[k], o, 0)
 
+    wait_all(flow.at[0:2, 0:4, grid_rows, :], local_sem.at[first])
+    wait_all(flow.at[2, 0:4, grid_rows, :], local_sem.at[first + 1])
+    wait_all(level.at[0:4, grid_rows, :], local_sem.at[first + 2])
+    top, low = slice(ROW0, ROW0 + 8), slice(ROW0 + 56, ROW0 + 64)
+    above, below = slice(ROW0 - 8, ROW0), slice(ROW0 + 64, ROW0 + 72)
+    group = lane // 8
+
+    def column(ring, t):
+        res = None
+        for r in range(8):
+            val = ring[t, ROW0 + 8 * r : ROW0 + 8 * r + 8, :]
+            turn = (8 * r + (8 if t else 0)) % LANES
+            val = pltpu.roll(val, turn, 1) if turn else val
+            res = val if res is None else jnp.where(group == r, val, res)
+        return res
+
+    corners = ((0, top), (3, top), (0, low), (3, low))
+    for side, t in ((0, 0), (1, 3)):
+        fx, fy, dp = (column(flow.at[k], t) for k in range(3))
+        flow_side[side, 0] = jnp.where(lane < 64, fx, pltpu.roll(fy, 64, 1))
+        flow_side[side, 1] = dp
+    for k, (t, rows) in enumerate(corners):
+        turns = (0, 8, 16) if t == 0 else (0, LANES - 8, LANES - 16)
+        fx, fy, dp = (
+            pltpu.roll(flow[i, t, rows, :], turns[i], 1) if i else flow[i, t, rows, :]
+            for i in range(3)
+        )
+        spot = group if t == 0 else 15 - group
+        flow_corner[k] = jnp.where(spot == 0, fx, jnp.where(spot == 1, fy, dp))
+    corner_offsets = (-n_tile - 1, -n_tile + 1, n_tile - 1, n_tile + 1)
+    cols = slice(0, 4)
+    push(flow.at[:, cols, top, :], flow.at[:, cols, below, :], -n_tile, 2)
+    push(flow.at[:, cols, low, :], flow.at[:, cols, above, :], n_tile, 2)
+    push(flow_side.at[0], flow_side_in.at[0], -1, 2)
+    push(flow_side.at[1], flow_side_in.at[1], 1, 2)
+    for k, o in enumerate(corner_offsets):
+        push(flow_corner.at[k], flow_corner_in.at[k], o, 2)
+
     near["send"].wait()
     sidx[...] = jnp.zeros_like(sidx)
     sidx[0:11, 0:SLOTS] = send[...]
-    def gather(sources, idx, tiles):
-        at, which = idx & (LANES - 1), idx >> 7
-        res = [jnp.zeros((8, LANES), F32)] * len(sources)
-        for t in tiles:
-            mask = which == t
-            for k, source in enumerate(sources):
-                val = jnp.take_along_axis(source[:, t * LANES : (t + 1) * LANES], at, axis=1)
-                res[k] = jnp.where(mask, val, res[k])
-        return res
-
-    direct = range(TILES)
-    pair = sub // 2
     block = lane // SLOTS
     places = [(v // 4, v % 4) for v in range(Q)] + [(2, 1 + j) for j in range(3)]
     rows = []
@@ -353,45 +410,7 @@
         for n in members:
             push(msg.at[n], msg_in.at[n], offsets[n], 1)
 
-    wait_all(flow.at[0:2, 0:4, grid_rows, :], local_sem.at[first])
-    wait_all(flow.at[2, 0:4, grid_rows, :], local_sem.at[first + 1])
-    wait_all(level.at[0:4, grid_rows, :], local_sem.at[first + 2])
-    top, low = slice(ROW0, ROW0 + 8), slice(ROW0 + 56, ROW0 + 64)
-    above, below = slice(ROW0 - 8, ROW0), slice(ROW0 + 64, ROW0 + 72)
-    group = lane // 8
-
-    def column(ring, t):
-        res = None
-        for r in range(8):
-            val = ring[t, ROW0 + 8 * r : ROW0 + 8 * r + 8, :]
-            turn = (8 * r + (8 if t else 0)) % LANES
-            val = pltpu.roll(val, turn, 1) if turn else val
-            res = val if res is None else jnp.where(group == r, val, res)
-        return res
-
-    corners = ((0, top), (3, top), (0, low), (3, low))
-    for side, t in ((0, 0), (1, 3)):
-        fx, fy, dp = (column(flow.at[k], t) for k in range(3))
-        flow_side[side, 0] = jnp.where(lane < 64, fx, pltpu.roll(fy, 64, 1))
-        flow_side[side, 1] = dp
-    for k, (t, rows) in enumerate(corners):
-        turns = (0, 8, 16) if t == 0 else (0, LANES - 8, LANES - 16)
-        fx, fy, dp = (
-            pltpu.roll(flow[i, t, rows, :], turns[i], 1) if i else flow[i, t, rows, :]
-            for i in range(3)
-        )
-        spot = group if t == 0 else 15 - group
-        flow_corner[k] = jnp.where(spot == 0, fx, jnp.where(spot == 1, fy, dp))
-    corner_offsets = (-n_tile - 1, -n_tile + 1, n_tile - 1, n_tile + 1)
-    cols = slice(0, 4)
-    push(flow.at[:, cols, top, :], flow.at[:, cols, below, :], -n_tile, 2)
-    push(flow.at[:, cols, low, :], flow.at[:, cols, above, :], n_tile, 2)
-    push(flow_side.at[0], flow_side_in.at[0], -1, 2)
-    push(flow_side.at[1], flow_side_in.at[1], 1, 2)
-    for k, o in enumerate(corner_offsets):
-        push(flow_corner.at[k], flow_corner_in.at[k], o, 2)
-
-    for name in ("nbr", "nrm", "fscale", "cluster", "sea_cell", "lift"):
+    for name in ("nrm", "fscale", "cluster", "sea_cell", "lift"):
         near[name].wait()
     lmat[...] = jnp.zeros_like(lmat)
     for f in range(4):
@@ -415,26 +434,6 @@
     for k, c in enumerate(coefs):
         for f in range(4):
             coef[k, 2 * f : 2 * f + 2, :] = jnp.broadcast_to(c[f : f + 1, :], (2, E))
-    for f in range(4):
-        nbr8[2 * f : 2 * f + 2, :] = jnp.broadcast_to(nbr[f : f + 1, :], (2, E))
-    def index(f, cut):
-        if f < 4:
-            return jnp.broadcast_to(nbr[f : f + 1, cut], (8, LANES))
-        return nbr8[:, cut]
-
-    def local_gather(i, _):
-        for et in range(AHEAD):
-            off = pl.multiple_of((i * AHEAD + et) * LANES, LANES)
-            cut = pl.ds(off, LANES)
-            for f in range(5):
-                here = pl.ds(pl.multiple_of(f * E + off, LANES), LANES)
-                got = gather([tab.at[v + Q * (f // 4)] for v in range(Q)], index(f, cut), direct)
-                for v in range(Q):
-                    acc[v, :, here] = got[v] - (tab[v, :, here] if f < 4 else otail[v, :, cut])
-        return 0
-
-    lax.fori_loop(0, 2 // AHEAD, local_gather, 0)
-
     wait_all(hand_in, recv_sem.at[0])
     back = (0, devices - 1, devices - n_tile, devices // 2)
     cells = pltpu.roll(sea_cell[...], shift, 1)
@@ -476,7 +475,7 @@
     for k, (o, (t, rows)) in enumerate(zip(corner_offsets, corners)):
         push(level.at[t, rows, :], level_corner_in.at[k], o, 3)
 
-    lax.fori_loop(2 // AHEAD, 4 // AHEAD, local_gather, 0)
+    lax.fori_loop(ahead, E // LANES, local_gather, 0)
 
     halo_bytes = flow.at[0, 0:4, 0:64, :]
     wait_all(halo_bytes, recv_sem.at[2])
@@ -610,7 +609,7 @@
 
 
 def grid_kernel(n_dom, n_tile, dof, flow_in, level_in, dof_out, height_out, momentum_out, *rest):
-    flow, level, sem = rest
+    flow, level, flow_res, sem = rest
     dof_copy = pltpu.make_async_copy(dof, dof_out, sem.at[0])
     dof_copy.start()
     above_ok, below_ok, right_ok, left_ok = inside(n_dom, n_tile)
@@ -644,16 +643,18 @@
 
     def push(r, flow_old, last=False):
         at, rows = block(r)
+        to, spot = (flow_res, slice(8 * r - 8, 8 * r)) if last else (flow, rows)
         vals = [level[t, rows, :] for t in range(5)]
         before = turned(vals, -2)
         res = []
         for t in range(5):
             if t < 4 or not last:
                 slope = level[t, at + 1 : at + 9, :] - level[t, at - 1 : at + 7, :]
-                flow[0, t, rows, :] = flow_old[0, t, rows, :] - flow_in[2, t, rows, :] * slope
+                to[0, t, spot, :] = flow_old[0, t, rows, :] - flow_in[2, t, rows, :] * slope
             res.append(flow_old[1, t, rows, :] - flow_in[3, t, rows, :] * (vals[t] - before[t]))
-        for t, val in enumerate(turned(res, 1) if last else res):
-            flow[1, t, rows, :] = val
+        res = turned(res, 1)[0:4] if last else res
+        for t, val in enumerate(res):
+            to[1, t, spot, :] = val
 
     def wave(flow_old, level_old):
         for r in range(10):
@@ -670,25 +671,24 @@
     lax.fori_loop(0, STEPS - 2, again, 0)
     for r in range(10):
         rise(r, flow, level)
-    copies = [dof_copy]
-
-    def send(src, dst):
-        copies.append(pltpu.make_async_copy(src, dst, sem.at[len(copies)]))
-        copies[-1].start()
-
     for t in range(4):
         lanes = slice(t * LANES, (t + 1) * LANES)
-        send(level.at[t, ROW0 : ROW0 + 64, :], height_out.at[:, lanes])
+        pltpu.make_async_copy(
+            level.at[t, ROW0 : ROW0 + 64, :], height_out.at[:, lanes], sem.at[1]
+        ).start()
     for part in range(2):
         for r in range(4 * part, 4 * part + 4):
             push(r + 1, flow, last=True)
         rows = slice(32 * part, 32 * part + 32)
         for t in range(4):
             lanes = slice(t * LANES, (t + 1) * LANES)
-            ring = slice(ROW0 + 32 * part, ROW0 + 32 * part + 32)
-            send(flow.at[:, t, ring, :], momentum_out.at[:, rows, lanes])
-    for c in copies:
-        c.wait()
+            pltpu.make_async_copy(
+                flow_res.at[:, t, rows, :], momentum_out.at[:, rows, lanes], sem.at[2]
+            ).start()
+    dof_copy.wait()
+    whole = level.at[0:4, ROW0 : ROW0 + 64, :]
+    pltpu.make_async_copy(whole, whole, sem.at[1]).wait()
+    pltpu.make_async_copy(flow_res, flow_res, sem.at[2]).wait()
 
 
 def shards(
@@ -791,7 +791,8 @@
         scratch_shapes=[
             pltpu.VMEM((2, 5, ROWS, LANES), F32),
             pltpu.VMEM((5, ROWS, LANES), F32),
-            pltpu.SemaphoreType.DMA((13,)),
+            pltpu.VMEM((2, 4, 64, LANES), F32),
+            pltpu.SemaphoreType.DMA((3,)),
         ],
         compiler_params=pltpu.CompilerParams(vmem_limit_bytes=16 << 20),
     )(dof_new, flow, level)

time: 19.9 us -> 19.3 us (0.970)
  Pallas kernels: 19.1 us -> 18.5 us
    pallas_call x1, Pallas kernels: 17.2 us -> 16.7 us  [shards(): pl.pallas_call(functools.partial(kernel, n_dom, n_tile), out_shape=(pltpu...]
where the time goes in v5:
time: 19.3 us; the launch traced here: 19.1 us
  Pallas kernels  18.5 us (96%)
  between operations  0.65 us (3%)
    pallas_call x1, Pallas kernels, shards(): pl.pallas_call(functools.partial(kernel, n_dom, n_tile), out_shape=(pltpu...  16.7 us
    pallas_call x1, Pallas kernels, shards(): pl.pallas_call(functools.partial(grid_kernel, n_dom, n_tile), out_shape=(...  1.79 us

profile of v5, /device:TPU:1, one launch (start us, length us, event | category | flops | bytes accessed | tf_op | source)
XLA Modules:
  0.0 19.1 jit_solution(10013176050486052341)
XLA Ops:
  0.6 16.7 %shard_map.193 = (f32[9,20,512]{2,1,0:T(8,128)S(1)}, f32[4,5,96,128]{3,2,1,0:T(8,128)S(1)}, f32[5,96,128]{2,1,0:T(8,128)S(1)}) custom-call(f32[9,20,512]{2,1,0:T(8,128)} %bitcast.11, f32[1,512]{1,0:T(1,128)} %bitcast.17, f32[1,512]{1,0:T(1,128)} %bitcast.18, f32[1,512]{1,0:T(1,128)} %bitcast.19, f32[3,3,512]{2,1,0:T(4,128)} %refs_4_.1, ...), custom_call_target="tpu_custom_call" | custom-call | tf_op jit(solution)/shard_map/pallas_call | solution.py:739
  17.3 1.8 %shard_map.194 = (f32[9,20,512]{2,1,0:T(8,128)}, f32[64,512]{1,0:T(8,128)}, f32[2,64,512]{2,1,0:T(8,128)}) custom-call(f32[9,20,512]{2,1,0:T(8,128)S(1)} %get-tuple-element.9.dof, f32[4,5,96,128]{3,2,1,0:T(8,128)S(1)} %get-tuple-element.10.flow_in, f32[5,96,128]{2,1,0:T(8,128)S(1)} %get-tuple-element.11.level_in), custom_call_target="tpu_custom_call" | custom-call | tf_op jit(solution)/shard_map/pallas_call | solution.py:782

commit v6 on v5

--- a/solution.py
+++ b/solution.py
@@ -107,6 +107,8 @@
         tails,
         hand,
         hand_in,
+        cell_rows,
+        cell_cols,
         flow,
         level,
         flow_side,
@@ -176,9 +178,9 @@
     lane = lax.broadcasted_iota(jnp.int32, (8, LANES), 1)
     sub = lax.broadcasted_iota(jnp.int32, (8, LANES), 0)
 
+    amat[...] = jnp.zeros_like(amat)
     for name in ("deriv", "fproj"):
         near[name].wait()
-    amat[...] = jnp.zeros_like(amat)
     for d in range(3):
         amat[d * BP : d * BP + B, 0:B] = deriv[d]
     for f in range(4):
@@ -434,35 +436,35 @@
     for k, c in enumerate(coefs):
         for f in range(4):
             coef[k, 2 * f : 2 * f + 2, :] = jnp.broadcast_to(c[f : f + 1, :], (2, E))
-    wait_all(hand_in, recv_sem.at[0])
     back = (0, devices - 1, devices - n_tile, devices // 2)
     cells = pltpu.roll(sea_cell[...], shift, 1)
     cells_t = jnp.transpose(
         jnp.concatenate([cells, jnp.zeros((64, LANES), jnp.int32)], axis=0).astype(F32)
     ).astype(jnp.int32)
+    row_ids = lax.broadcasted_iota(jnp.int32, (64, LANES), 0)
+    col_ids = lax.broadcasted_iota(jnp.int32, (64, E), 1)
+    for k in range(0, 4, 2):
+        pair_c = cells_t[back[k] : back[k] + 1, :] + pltpu.roll(
+            cells_t[back[k + 1] : back[k + 1] + 1, :], 64, 1
+        )
+        here = row_ids == jnp.broadcast_to(pair_c >> 9, (64, LANES))
+        cell_rows[k // 2] = jnp.where(here, 1.0, 0.0)
+    for k in range(4):
+        chosen = jnp.broadcast_to(cells[:, back[k] : back[k] + 1] & (E - 1), (64, E))
+        cell_cols[64 * k : 64 * k + 64, :] = jnp.where(col_ids == chosen, 1.0, 0.0).astype(BF16)
+    wait_all(hand_in, recv_sem.at[0])
     values = [hand[0:1, :]]
     for k, o in enumerate(hand_offsets):
         values.append(hand_in[k, o % 8 : o % 8 + 1, :])
-    row_ids = lax.broadcasted_iota(jnp.int32, (64, LANES), 0)
     highs, lows = [], []
     for k in range(0, 4, 2):
-        pair_v = values[k] + pltpu.roll(values[k + 1], 64, 1)
-        pair_c = cells_t[back[k] : back[k] + 1, :] + pltpu.roll(
-            cells_t[back[k + 1] : back[k + 1] + 1, :], 64, 1
-        )
-        v_high, v_low = split(pair_v)
-        here = row_ids == jnp.broadcast_to(pair_c >> 9, (64, LANES))
-        highs.append(jnp.where(here, v_high, 0.0))
-        lows.append(jnp.where(here, v_low, 0.0))
+        v_high, v_low = split(values[k] + pltpu.roll(values[k + 1], 64, 1))
+        highs.append(cell_rows[k // 2] * v_high)
+        lows.append(cell_rows[k // 2] * v_low)
     left = jnp.concatenate(
         [jnp.concatenate(highs, axis=1), jnp.concatenate(lows, axis=1)], axis=0
     ).astype(BF16)
-    col_ids = lax.broadcasted_iota(jnp.int32, (64, E), 1)
-    picks = []
-    for k in range(4):
-        chosen = jnp.broadcast_to(cells[:, back[k] : back[k] + 1] & (E - 1), (64, E))
-        picks.append(jnp.where(col_ids == chosen, 1.0, 0.0).astype(BF16))
-    lifted = jnp.dot(left, jnp.concatenate(picks, axis=0), preferred_element_type=F32)
+    lifted = jnp.dot(left, cell_cols[...], preferred_element_type=F32)
     for t in range(4):
         lanes = slice(t * LANES, (t + 1) * LANES)
         level[t, ROW0 : ROW0 + 64, :] += lifted[0:64, lanes] + lifted[64:128, lanes]
@@ -762,6 +764,8 @@
             pltpu.VMEM((9, 8, LANES), F32),
             pltpu.VMEM((LANES, LANES), F32),
             pltpu.VMEM((3, 8, LANES), F32),
+            pltpu.VMEM((2, 64, LANES), F32),
+            pltpu.VMEM((256, E), BF16),
             pltpu.VMEM((3, 5, ROWS, LANES), F32),
             pltpu.VMEM((5, ROWS, LANES), F32),
             pltpu.VMEM((2, 2, 8, LANES), F32),

time: 19.3 us -> 19.1 us (0.990)
  Pallas kernels: 18.5 us -> 18.3 us
    pallas_call x1, Pallas kernels: 16.7 us -> 16.5 us  [shards(): pl.pallas_call(functools.partial(kernel, n_dom, n_tile), out_shape=(pltpu...]
where the time goes in v6:
time: 19.1 us; the launch traced here: 18.9 us
  Pallas kernels  18.3 us (96%)
  between operations  0.65 us (3%)
    pallas_call x1, Pallas kernels, shards(): pl.pallas_call(functools.partial(kernel, n_dom, n_tile), out_shape=(pltpu...  16.5 us
    pallas_call x1, Pallas kernels, shards(): pl.pallas_call(functools.partial(grid_kernel, n_dom, n_tile), out_shape=(...  1.79 us

profile of v6, /device:TPU:1, one launch (start us, length us, event | category | flops | bytes accessed | tf_op | source)
XLA Modules:
  0.0 18.9 jit_solution(16403893366664806503)
XLA Ops:
  0.6 16.5 %shard_map.193 = (f32[9,20,512]{2,1,0:T(8,128)S(1)}, f32[4,5,96,128]{3,2,1,0:T(8,128)S(1)}, f32[5,96,128]{2,1,0:T(8,128)S(1)}) custom-call(f32[9,20,512]{2,1,0:T(8,128)} %bitcast.11, f32[1,512]{1,0:T(1,128)} %bitcast.17, f32[1,512]{1,0:T(1,128)} %bitcast.18, f32[1,512]{1,0:T(1,128)} %bitcast.19, f32[3,3,512]{2,1,0:T(4,128)} %refs_4_.1, ...), custom_call_target="tpu_custom_call" | custom-call | tf_op jit(solution)/shard_map/pallas_call | solution.py:741
  17.1 1.8 %shard_map.194 = (f32[9,20,512]{2,1,0:T(8,128)}, f32[64,512]{1,0:T(8,128)}, f32[2,64,512]{2,1,0:T(8,128)}) custom-call(f32[9,20,512]{2,1,0:T(8,128)S(1)} %get-tuple-element.9.dof, f32[4,5,96,128]{3,2,1,0:T(8,128)S(1)} %get-tuple-element.10.flow_in, f32[5,96,128]{2,1,0:T(8,128)S(1)} %get-tuple-element.11.level_in), custom_call_target="tpu_custom_call" | custom-call | tf_op jit(solution)/shard_map/pallas_call | solution.py:786
